TPU v7x, 32 devices: a whole 2x2x4 slice. The times are simulated.
32 devices in a mesh: dp: 8 (over z, x), shard: 4 (over y, core).
Axes of the slice: x: 2, y: 2, z: 4, core: 2. Of those that a mesh axis runs over, the one named last changes fastest.
Arguments:
- target: bfloat16 [32, 1024, 512], P(('dp', 'shard')), may hold values from -6 to 6
- memory: bfloat16 [32, 1024, 512], P(('dp', 'shard')), may hold values from -6 to 6
- cotangent: bfloat16 [32, 1024, 512], P(('dp', 'shard')), may hold values from -6 to 6
- target_lengths: int32 [32, 24], P(('dp', 'shard')), may hold values from 1 to 512, 1024 in all within a row
- source_lengths: int32 [32, 24], P(('dp', 'shard')), may hold values from 1 to 512, 1024 in all within a row
- inward_master: float32 [1572864], P(('dp', 'shard')), may hold values from -0.25 to 0.25
- inward_mean: float32 [1572864], P(('dp', 'shard')), may hold values from -320 to 320
- inward_square: float32 [1572864], P(('dp', 'shard')), may hold values from 327.68 to 32768
- outward_master: float32 [524288], P(('dp', 'shard')), may hold values from -0.75 to 0.75
- outward_mean: float32 [524288], P(('dp', 'shard')), may hold values from -320 to 320
- outward_square: float32 [524288], P(('dp', 'shard')), may hold values from 327.68 to 32768
- expand_master: float32 [1048576], P(('dp', 'shard')), may hold values from -0.25 to 0.25
- expand_mean: float32 [1048576], P(('dp', 'shard')), may hold values from -320 to 320
- expand_square: float32 [1048576], P(('dp', 'shard')), may hold values from 327.68 to 32768
- shrink_master: float32 [1048576], P(('dp', 'shard')), may hold values from -0.125 to 0.125
- shrink_mean: float32 [1048576], P(('dp', 'shard')), may hold values from -320 to 320
- shrink_square: float32 [1048576], P(('dp', 'shard')), may hold values from 327.68 to 32768
- norms_master: float32 [3072], P(('dp', 'shard')), may hold values from -0.5 to 1.3, as said below
- norms_mean: float32 [3072], P(('dp', 'shard')), may hold values from -320 to 320
- norms_square: float32 [3072], P(('dp', 'shard')), may hold values from 327.68 to 32768
Outputs:
- result: bfloat16 [32, 1024, 512], P(('dp', 'shard'))
- target_grad: float32 [32, 1024, 512], P(('dp', 'shard'))
- memory_grad: float32 [32, 1024, 512], P(('dp', 'shard'))
- change_inward: float32 [1572864], P(('dp', 'shard'))
- mean_inward: float32 [1572864], P(('dp', 'shard'))
- summed_inward: float32 [1572864], P(('dp', 'shard'))
- change_outward: float32 [524288], P(('dp', 'shard'))
- mean_outward: float32 [524288], P(('dp', 'shard'))
- summed_outward: float32 [524288], P(('dp', 'shard'))
- change_expand: float32 [1048576], P(('dp', 'shard'))
- mean_expand: float32 [1048576], P(('dp', 'shard'))
- summed_expand: float32 [1048576], P(('dp', 'shard'))
- change_shrink: float32 [1048576], P(('dp', 'shard'))
- mean_shrink: float32 [1048576], P(('dp', 'shard'))
- summed_shrink: float32 [1048576], P(('dp', 'shard'))
- change_norms: float32 [3072], P(('dp', 'shard'))
- mean_norms: float32 [3072], P(('dp', 'shard'))
- summed_norms: float32 [3072], P(('dp', 'shard'))
Inputs may be any that keep to these rules, and one draw needn't show every extreme that they name: `target_lengths`: in each row the 24 lengths sum to 1024; the last entry is padding, the others are sentences; target sentence i is the translation of source sentence i. `source_lengths`: as target_lengths, for the source side. `norms_master`: the first 1536 entries are gains, the others biases.
All inputs are finite; a program needn't handle non-finite values.
Results may differ from a plain program's by a relative error of at most 0.015.
The roundings to bfloat16 on the way count: a program that leaves them out, or rounds other values in their place, can miss the bound.
Values may be sent and summed in bfloat16 or wider, within the bound.
A program may use at most 192 MiB of HBM per device.

v0:
```python
import jax
import jax.numpy as jnp
from jax import lax
from jax.sharding import PartitionSpec as P

D = 512
HEADS = 8
HD = 64
FF = 2048
ROW = 1024
SEGS = 24
STEP = 10


learn_rate = 0.001
beta_one = 0.9
beta_two = 0.999


def matmul(left_mat, right_mat):
    return jnp.dot(left_mat, right_mat, preferred_element_type=jnp.float32)


def left_dot(left_mat, right_mat):
    return lax.dot_general(
        left_mat, right_mat, (((0,), (0,)), ((), ())), preferred_element_type=jnp.float32
    )


def right_dot(left_mat, right_mat):
    return lax.dot_general(
        left_mat, right_mat, (((1,), (1,)), ((), ())), preferred_element_type=jnp.float32
    )


def layer_norm(residual, norm_gain, norm_bias):
    centered = residual - jnp.mean(residual, -1, keepdims=True)
    spread = jnp.mean(centered * centered, -1, keepdims=True)
    return centered * lax.rsqrt(spread + 1e-05) * norm_gain + norm_bias


def segments(lengths):
    ends = jnp.cumsum(lengths, axis=-1)
    places = jnp.arange(ROW, dtype=jnp.int32)
    return jnp.sum((places[None, :, None] >= ends[:, None, :]).astype(jnp.int32), -1)


def pair_mask(query_seg, key_seg, row_start, causal):
    allowed = query_seg[:, None] == key_seg[None, :]
    if causal:
        query_pos = row_start + jnp.arange(query_seg.shape[0], dtype=jnp.int32)
        key_pos = jnp.arange(key_seg.shape[0], dtype=jnp.int32)
        allowed = allowed & (key_pos[None, :] <= query_pos[:, None])
    return allowed


def attend(queries, keys, values, query_seg, key_seg, causal):
    block_rows = min(512, queries.shape[1])
    block_count = queries.shape[1] // block_rows
    score_scale = queries.shape[3] ** (-0.5)

    def one_row(row_items):
        q_row, k_row, v_row, qs_row, ks_row = row_items

        def one_block(block_index):
            row_start = block_index * block_rows
            q_block = lax.dynamic_slice_in_dim(q_row, row_start, block_rows, 0)
            seg_block = lax.dynamic_slice_in_dim(qs_row, row_start, block_rows, 0)
            scores = (
                jnp.einsum("qhd,khd->hqk", q_block, k_row, preferred_element_type=jnp.float32)
                * score_scale
            )
            allowed = pair_mask(seg_block, ks_row, row_start, causal)
            scores = jnp.where(allowed[None], scores, -1000000000.0)
            row_peak = jnp.max(scores, -1, keepdims=True)
            raised = jnp.exp(scores - row_peak)
            row_total = jnp.sum(raised, -1, keepdims=True)
            probs = (raised / row_total).astype(jnp.bfloat16)
            context = jnp.einsum("hqk,khd->qhd", probs, v_row, preferred_element_type=jnp.float32)
            return (context, row_peak[..., 0] + jnp.log(row_total[..., 0]))

        context, logsum = lax.map(one_block, jnp.arange(block_count, dtype=jnp.int32))
        return (context.reshape(-1, q_row.shape[1] * q_row.shape[2]), logsum)

    return lax.map(one_row, (queries, keys, values, query_seg, key_seg))


def attend_back(queries, keys, values, logsum, grad_ctx, query_seg, key_seg, causal):
    block_rows = min(512, queries.shape[1])
    block_count = queries.shape[1] // block_rows
    score_scale = queries.shape[3] ** (-0.5)

    def one_row(row_items):
        q_row, k_row, v_row, ls_row, g_row, qs_row, ks_row = row_items

        def one_block(carry, block_index):
            grad_keys, grad_values = carry
            row_start = block_index * block_rows
            q_block = lax.dynamic_slice_in_dim(q_row, row_start, block_rows, 0)
            g_block = lax.dynamic_slice_in_dim(g_row, row_start, block_rows, 0)
            seg_block = lax.dynamic_slice_in_dim(qs_row, row_start, block_rows, 0)
            ls_block = lax.dynamic_index_in_dim(ls_row, block_index, 0, keepdims=False)
            scores = (
                jnp.einsum("qhd,khd->hqk", q_block, k_row, preferred_element_type=jnp.float32)
                * score_scale
            )
            allowed = pair_mask(seg_block, ks_row, row_start, causal)
            probs = jnp.where(allowed[None], jnp.exp(scores - ls_block[..., None]), 0.0)
            grad_probs = jnp.einsum(
                "qhd,khd->hqk", g_block, v_row, preferred_element_type=jnp.float32
            )
            inner = jnp.sum(probs * grad_probs, -1, keepdims=True)
            grad_scores = (probs * (grad_probs - inner) * score_scale).astype(jnp.bfloat16)
            grad_query = jnp.einsum(
                "hqk,khd->qhd", grad_scores, k_row, preferred_element_type=jnp.float32
            )
            grad_keys = grad_keys + jnp.einsum(
                "hqk,qhd->khd", grad_scores, q_block, preferred_element_type=jnp.float32
            )
            grad_values = grad_values + jnp.einsum(
                "hqk,qhd->khd",
                probs.astype(jnp.bfloat16),
                g_block,
                preferred_element_type=jnp.float32,
            )
            return ((grad_keys, grad_values), grad_query)

        empty = jnp.zeros(k_row.shape, jnp.float32)
        (grad_keys, grad_values), grad_query = lax.scan(
            one_block, (empty, empty), jnp.arange(block_count, dtype=jnp.int32)
        )
        return (grad_query.reshape(q_row.shape), grad_keys, grad_values)

    return lax.map(one_row, (queries, keys, values, logsum, grad_ctx, query_seg, key_seg))


def unpack(inward_all, outward_all, norms_all, expand_all, shrink_all):
    norm_par = norms_all.reshape(2, 3, D).astype(jnp.float32)
    return (
        inward_all.reshape(6, D, D),
        outward_all.reshape(2, D, D),
        expand_all.reshape(D, FF),
        shrink_all.reshape(FF, D),
        norm_par[0],
        norm_par[1],
    )


def adam_step(mean_old, square_old, grad_share):
    mean_new = beta_one * mean_old + (1.0 - beta_one) * grad_share
    square_new = beta_two * square_old + (1.0 - beta_two) * grad_share * grad_share
    steps_float = float(STEP)
    mean_hat = mean_new / (1.0 - beta_one**steps_float)
    square_hat = square_new / (1.0 - beta_two**steps_float)
    change = -learn_rate * mean_hat / (jnp.sqrt(square_hat) + 1e-08)
    return (change, mean_new, grad_share)


def body(
    target,
    memory,
    cotangent,
    target_lengths,
    source_lengths,
    inward_master,
    inward_mean,
    inward_square,
    outward_master,
    outward_mean,
    outward_square,
    expand_master,
    expand_mean,
    expand_square,
    shrink_master,
    shrink_mean,
    shrink_square,
    norms_master,
    norms_mean,
    norms_square,
):
    row_count = target.shape[0]
    inward_low = inward_master.astype(jnp.bfloat16)
    outward_low = outward_master.astype(jnp.bfloat16)
    expand_low = expand_master.astype(jnp.bfloat16)
    shrink_low = shrink_master.astype(jnp.bfloat16)
    norms_low = norms_master.astype(jnp.bfloat16)
    inward_all, outward_all, norms_all = (
        lax.all_gather(inward_low, ("dp", "shard"), axis=0, tiled=True),
        lax.all_gather(outward_low, ("dp", "shard"), axis=0, tiled=True),
        lax.all_gather(norms_low, ("dp", "shard"), axis=0, tiled=True),
    )
    expand_all, shrink_all = (
        lax.all_gather(expand_low, ("dp", "shard"), axis=0, tiled=True),
        lax.all_gather(shrink_low, ("dp", "shard"), axis=0, tiled=True),
    )
    w_in, w_out, w_up, w_down, gains, biases = unpack(
        inward_all, outward_all, norms_all, expand_all, shrink_all
    )
    target_seg = segments(target_lengths)
    source_seg = segments(source_lengths)
    live_rows = (target_seg < SEGS - 1).astype(jnp.float32).reshape(-1, 1)

    def heads(values_flat):
        return values_flat.reshape(row_count, ROW, HEADS, HD)

    tokens = target.reshape(-1, D)
    source = memory.reshape(-1, D)
    query_one = matmul(tokens, w_in[0]).astype(jnp.bfloat16)
    key_one = matmul(tokens, w_in[1]).astype(jnp.bfloat16)
    value_one = matmul(tokens, w_in[2]).astype(jnp.bfloat16)
    ctx_raw, logsum_one = attend(
        heads(query_one), heads(key_one), heads(value_one), target_seg, target_seg, True
    )
    ctx_one = ctx_raw.reshape(-1, D).astype(jnp.bfloat16)
    resid_one = tokens.astype(jnp.float32) + matmul(ctx_one, w_out[0])
    hidden_one = layer_norm(resid_one, gains[0], biases[0])
    hidden_low = hidden_one.astype(jnp.bfloat16)
    query_two = matmul(hidden_low, w_in[3]).astype(jnp.bfloat16)
    key_two = matmul(source, w_in[4]).astype(jnp.bfloat16)
    value_two = matmul(source, w_in[5]).astype(jnp.bfloat16)
    ctx_raw, logsum_two = attend(
        heads(query_two), heads(key_two), heads(value_two), target_seg, source_seg, False
    )
    ctx_two = ctx_raw.reshape(-1, D).astype(jnp.bfloat16)
    resid_two = hidden_one + matmul(ctx_two, w_out[1])
    hidden_two = layer_norm(resid_two, gains[1], biases[1])
    second_low = hidden_two.astype(jnp.bfloat16)
    pre_act = matmul(second_low, w_up)
    activated = jax.nn.silu(pre_act).astype(jnp.bfloat16)
    resid_three = hidden_two + matmul(activated, w_down)
    output = layer_norm(resid_three, gains[2], biases[2])
    inward_back, outward_back, norms_back, expand_back, shrink_back = (
        lax.all_gather(inward_low, ("dp", "shard"), axis=0, tiled=True),
        lax.all_gather(outward_low, ("dp", "shard"), axis=0, tiled=True),
        lax.all_gather(norms_low, ("dp", "shard"), axis=0, tiled=True),
        lax.all_gather(expand_low, ("dp", "shard"), axis=0, tiled=True),
        lax.all_gather(shrink_low, ("dp", "shard"), axis=0, tiled=True),
    )
    w_in, w_out, w_up, w_down, gains, biases = unpack(
        inward_back, outward_back, norms_back, expand_back, shrink_back
    )
    seed = cotangent.reshape(-1, D).astype(jnp.float32) * live_rows
    _, pull_three = jax.vjp(layer_norm, resid_three, gains[2], biases[2])
    grad_three, gain_three, bias_three = pull_three(seed)
    grad_out = grad_three.astype(jnp.bfloat16)
    grad_shrink = left_dot(activated, grad_out)
    grad_act = right_dot(grad_out, w_down)
    _, pull_act = jax.vjp(jax.nn.silu, pre_act)
    grad_pre = pull_act(grad_act)[0].astype(jnp.bfloat16)
    grad_expand = left_dot(second_low, grad_pre)
    grad_hidden_two = grad_three + right_dot(grad_pre, w_up)
    _, pull_two = jax.vjp(layer_norm, resid_two, gains[1], biases[1])
    grad_two, gain_two, bias_two = pull_two(grad_hidden_two)
    branch_two = grad_two.astype(jnp.bfloat16)
    grad_wo_two = left_dot(ctx_two, branch_two)
    grad_ctx_two = right_dot(branch_two, w_out[1]).astype(jnp.bfloat16)
    dq_two, dk_two, dv_two = attend_back(
        heads(query_two),
        heads(key_two),
        heads(value_two),
        logsum_two,
        heads(grad_ctx_two),
        target_seg,
        source_seg,
        False,
    )
    dq_two = dq_two.reshape(-1, D).astype(jnp.bfloat16)
    dk_two = dk_two.reshape(-1, D).astype(jnp.bfloat16)
    dv_two = dv_two.reshape(-1, D).astype(jnp.bfloat16)
    grad_wq_two = left_dot(hidden_low, dq_two)
    grad_wk_two = left_dot(source, dk_two)
    grad_wv_two = left_dot(source, dv_two)
    memory_grad = right_dot(dk_two, w_in[4]) + right_dot(dv_two, w_in[5])
    grad_hidden_one = grad_two + right_dot(dq_two, w_in[3])
    _, pull_one = jax.vjp(layer_norm, resid_one, gains[0], biases[0])
    grad_one, gain_one, bias_one = pull_one(grad_hidden_one)
    branch_one = grad_one.astype(jnp.bfloat16)
    grad_wo_one = left_dot(ctx_one, branch_one)
    grad_ctx_one = right_dot(branch_one, w_out[0]).astype(jnp.bfloat16)
    dq_one, dk_one, dv_one = attend_back(
        heads(query_one),
        heads(key_one),
        heads(value_one),
        logsum_one,
        heads(grad_ctx_one),
        target_seg,
        target_seg,
        True,
    )
    dq_one = dq_one.reshape(-1, D).astype(jnp.bfloat16)
    dk_one = dk_one.reshape(-1, D).astype(jnp.bfloat16)
    dv_one = dv_one.reshape(-1, D).astype(jnp.bfloat16)
    grad_wq_one = left_dot(tokens, dq_one)
    grad_wk_one = left_dot(tokens, dk_one)
    grad_wv_one = left_dot(tokens, dv_one)
    target_grad = (
        grad_one
        + right_dot(dq_one, w_in[0])
        + right_dot(dk_one, w_in[1])
        + right_dot(dv_one, w_in[2])
    )
    grad_inward = jnp.stack(
        [grad_wq_one, grad_wk_one, grad_wv_one, grad_wq_two, grad_wk_two, grad_wv_two]
    ).reshape(-1)
    grad_outward = jnp.stack([grad_wo_one, grad_wo_two]).reshape(-1)
    grad_norms = jnp.stack(
        [jnp.stack([gain_one, gain_two, gain_three]), jnp.stack([bias_one, bias_two, bias_three])]
    ).reshape(-1)
    inward_share, outward_share, norms_share, expand_share, shrink_share = (
        lax.psum_scatter(grad_inward, ("dp", "shard"), scatter_dimension=0, tiled=True),
        lax.psum_scatter(grad_outward, ("dp", "shard"), scatter_dimension=0, tiled=True),
        lax.psum_scatter(grad_norms, ("dp", "shard"), scatter_dimension=0, tiled=True),
        lax.psum_scatter(grad_expand.reshape(-1), ("dp", "shard"), scatter_dimension=0, tiled=True),
        lax.psum_scatter(grad_shrink.reshape(-1), ("dp", "shard"), scatter_dimension=0, tiled=True),
    )
    in_c, in_m, in_g = adam_step(inward_mean, inward_square, inward_share)
    out_c, out_m, out_g = adam_step(outward_mean, outward_square, outward_share)
    up_c, up_m, up_g = adam_step(expand_mean, expand_square, expand_share)
    down_c, down_m, down_g = adam_step(shrink_mean, shrink_square, shrink_share)
    norm_c, norm_m, norm_g = adam_step(norms_mean, norms_square, norms_share)
    shape_rows = (row_count, ROW, D)
    return (
        output.astype(jnp.bfloat16).reshape(shape_rows),
        target_grad.reshape(shape_rows),
        memory_grad.reshape(shape_rows),
        in_c,
        in_m,
        in_g,
        out_c,
        out_m,
        out_g,
        up_c,
        up_m,
        up_g,
        down_c,
        down_m,
        down_g,
        norm_c,
        norm_m,
        norm_g,
    )


def solution(mesh):
    return jax.shard_map(
        body,
        mesh=mesh,
        in_specs=(
            P(("dp", "shard"), None, None),
            P(("dp", "shard"), None, None),
            P(("dp", "shard"), None, None),
            P(("dp", "shard"), None),
            P(("dp", "shard"), None),
            P(("dp", "shard")),
            P(("dp", "shard")),
            P(("dp", "shard")),
            P(("dp", "shard")),
            P(("dp", "shard")),
            P(("dp", "shard")),
            P(("dp", "shard")),
            P(("dp", "shard")),
            P(("dp", "shard")),
            P(("dp", "shard")),
            P(("dp", "shard")),
            P(("dp", "shard")),
            P(("dp", "shard")),
            P(("dp", "shard")),
            P(("dp", "shard")),
        ),
        out_specs=(
            P(("dp", "shard"), None, None),
            P(("dp", "shard"), None, None),
            P(("dp", "shard"), None, None),
            P(("dp", "shard")),
            P(("dp", "shard")),
            P(("dp", "shard")),
            P(("dp", "shard")),
            P(("dp", "shard")),
            P(("dp", "shard")),
            P(("dp", "shard")),
            P(("dp", "shard")),
            P(("dp", "shard")),
            P(("dp", "shard")),
            P(("dp", "shard")),
            P(("dp", "shard")),
            P(("dp", "shard")),
            P(("dp", "shard")),
            P(("dp", "shard")),
        ),
        check_vma=False,
    )
```

profile of v0, /device:TPU:0, one launch (start us, length us, event | category | flops | bytes accessed | tf_op | source)
XLA Modules:
  0.0 1016.5 jit_solution(18071916766514258898)
XLA Ops:
  17.8 42.1 %all-reduce = bf16[3072]{0:T(1024)(128)(2,1)S(1)} all-reduce(bf16[3072]{0:T(1024)(128)(2,1)S(1)} %dynamic-update-slice), channel_id=1, replica_groups=mesh['dp'=8,'shard'=4] {'dp','shard'}, use_global_device_ids=true, to_apply=%add | all-reduce | flops 3072 | bytes 12288
  64.1 4.2 all-gather.7.cloned.1.call-done
  71.8 55.1 %all-gather.9.cloned.1.call-done = bf16[1048576]{0:T(1024)(128)(2,1)} async-done(((bf16[32768]{0:T(1024)(128)(2,1)}), bf16[1048576]{0:T(1024)(128)(2,1)}) %all-gather.9.cloned.1.call-update) | async-done | bytes 2097168 | tf_op jit(solution)/shard_map/all_gather | solution.py:193
  126.9 4.2 reshape.655
  131.1 54.6 %all-gather.11.cloned.1.call-done = bf16[1048576]{0:T(1024)(128)(2,1)} async-done(((bf16[32768]{0:T(1024)(128)(2,1)}), bf16[1048576]{0:T(1024)(128)(2,1)}) %all-gather.11.cloned.1.call-update) | async-done | bytes 2097168 | tf_op jit(solution)/shard_map/all_gather | solution.py:194
  185.6 4.4 reshape.656
  190.0 56.9 %all-gather.5.cloned.1.call-done = bf16[1572864]{0:T(1024)(128)(2,1)} async-done(((bf16[49152]{0:T(1024)(128)(2,1)}), bf16[1572864]{0:T(1024)(128)(2,1)}) %all-gather.5.cloned.1.call-update) | async-done | bytes 3145744 | tf_op jit(solution)/shard_map/all_gather | solution.py:188
  246.9 3.0 fusion.159
  257.1 3.1 convolution_convert_fusion.7
  267.0 33.5 %while.96 = (s32[]{:T(128)}, bf16[2,512,8,64]{1,3,2,0:T(8,128)(2,1)}, f32[2,8,512]{2,1,0:T(8,128)S(1)}, s32[2]{0:T(128)S(1)}, s32[1024]{0:T(1024)S(1)}, /*index=...) while((s32[]{:T(128)}, ...), condition=%wide.region_5.6_spmd, body=%wide.region_2.0_spmd.sunk | while | flops 1125642752 | bytes 64633092 | solution.py:82
  269.2 4.1 fusion.257
  273.3 4.2 fusion.258
  277.5 5.4 fusion.259
  285.8 4.1 fusion.257
  289.9 4.2 fusion.258
  294.2 5.4 fusion.259
  300.5 3.1 copy.79
  309.4 41.3 %while.97 = (s32[]{:T(128)}, bf16[2,512,8,64]{1,3,2,0:T(8,128)(2,1)}, f32[2,8,512]{2,1,0:T(8,128)S(1)}, s32[2]{0:T(128)S(1)}, s32[1024]{0:T(1024)S(1)}, /*index=...) while((s32[]{:T(128)}, ...), condition=%wide.region_13.14_spmd, body=%wide.region_10.13_spmd.sunk | while | flops 1124593664 | bytes 64628996 | solution.py:82
  311.1 4.1 fusion.262
  315.2 4.2 fusion.263
  319.4 5.4 fusion.264
  327.5 4.1 fusion.262
  331.6 4.2 fusion.263
  335.8 5.4 fusion.264
  350.7 2.5 copy.80
  356.1 3.9 multiply_convert_fusion.2
  360.0 2.6 fusion.164
  363.4 2.7 fusion.105
  366.0 5.1 convolution_bitcast_fusion
  371.1 5.1 fusion.98
  376.2 4.1 multiply_reduce_fusion.2
  380.2 4.6 convolution_bitcast_fusion.1
  389.0 141.6 %while.98 = (s32[]{:T(128)}, f32[1024,8,64]{0,2,1:T(8,128)}, f32[1024,8,64]{0,2,1:T(8,128)}, bf16[2,512,8,64]{1,3,2,0:T(8,128)(2,1)}, s32[2]{0:T(128)S(1)}, /*in...) while((s32[]{:T(128)}, f32[1024,8,64]{0,2,1:T(8,128)}, ...), condition=%wide.region_24.25_spmd.clone, body=%wide.region_22.24_spmd.clone.sunk | while | flops 2745706496 | bytes 267446608 | solution.py:129
  393.0 5.8 exponential_select_fusion.4
  398.8 3.4 bitcast_add_fusion.9
  402.3 2.9 copy-done.1
  405.2 8.1 fusion.275
  413.3 22.7 %fusion.276 = bf16[2,512,8,64]{1,3,2,0:T(8,128)(2,1)} fusion(bf16[2,512,8,64]{1,3,2,0:T(8,128)(2,1)} %get-tuple-element.1065, s32[]{:T(128)S(6)} %copy.136, bf16[1024,8,64]{0,2,1:T(8,128)(2,1)} %get-tuple-element.1087, f32[8,512,1024]{2,1,0:T(8,128)} %copy-done.1, f32[8,512,1024]{2,1,0:T(8,128)} %fusion.275), kind=kOutput, calls=%fused_computation.46.clone.1 | convolution fusion | flops 557847552 | bytes 69206016 | tf_op jit(solution)/shard_map/while/body/eval_jaxpr/while/body/eval_jaxpr/hqk,khd->qhd/dot_general | solution.py:114
  436.0 23.4 %bitcast_add_fusion.8 = f32[1024,8,64]{0,2,1:T(8,128)} fusion(f32[1024,8,64]{0,2,1:T(8,128)} %get-tuple-element.1063, f32[8,512,1024]{2,1,0:T(8,128)} %copy-done.1, f32[8,512,1024]{2,1,0:T(8,128)} %fusion.275, pred[]{:T(512)S(6)} %compare.6, bf16[1024,8,64]{0,2,1:T(8,128)(2,1)} %get-tuple-element.1084, s32[]{:T(128)S(6)} %select_n.103), kind=kOutput, calls=%fused_computation.44.clone.1 | convolution fusion | flops 558896128 | bytes 71827464 | tf_op jit(solution)/shard_map/while/body/eval_jaxpr/while/body/eval_jaxpr/hqk,qhd->khd/dot_general | solution.py:117
  463.0 5.8 exponential_select_fusion.4
  468.8 6.4 bitcast_add_fusion.9
  475.8 8.1 fusion.275
  483.9 22.7 %fusion.276 = bf16[2,512,8,64]{1,3,2,0:T(8,128)(2,1)} fusion(bf16[2,512,8,64]{1,3,2,0:T(8,128)(2,1)} %get-tuple-element.1065, s32[]{:T(128)S(6)} %copy.136, bf16[1024,8,64]{0,2,1:T(8,128)(2,1)} %get-tuple-element.1087, f32[8,512,1024]{2,1,0:T(8,128)} %copy-done.1, f32[8,512,1024]{2,1,0:T(8,128)} %fusion.275), kind=kOutput, calls=%fused_computation.46.clone.1 | convolution fusion | flops 557847552 | bytes 69206016 | tf_op jit(solution)/shard_map/while/body/eval_jaxpr/while/body/eval_jaxpr/hqk,khd->qhd/dot_general | solution.py:114
  506.6 24.0 %bitcast_add_fusion.8 = f32[1024,8,64]{0,2,1:T(8,128)} fusion(f32[1024,8,64]{0,2,1:T(8,128)} %get-tuple-element.1063, f32[8,512,1024]{2,1,0:T(8,128)} %copy-done.1, f32[8,512,1024]{2,1,0:T(8,128)} %fusion.275, pred[]{:T(512)S(6)} %compare.6, bf16[1024,8,64]{0,2,1:T(8,128)(2,1)} %get-tuple-element.1084, s32[]{:T(128)S(6)} %select_n.103), kind=kOutput, calls=%fused_computation.44.clone.1 | convolution fusion | flops 558896128 | bytes 71827464 | tf_op jit(solution)/shard_map/while/body/eval_jaxpr/while/body/eval_jaxpr/hqk,qhd->khd/dot_general | solution.py:117
  530.7 2.5 copy.83
  533.5 3.4 multiply_reduce_fusion.3
  540.4 3.0 copy.105
  543.4 3.1 copy.106
  549.7 142.0 %while.99 = (s32[]{:T(128)}, f32[1024,8,64]{0,2,1:T(8,128)}, f32[1024,8,64]{0,2,1:T(8,128)}, bf16[2,512,8,64]{1,3,2,0:T(8,128)(2,1)}, s32[2]{0:T(128)S(1)}, /*in...) while((s32[]{:T(128)}, f32[1024,8,64]{0,2,1:T(8,128)}, ...), condition=%wide.region_29.30_spmd.clone, body=%wide.region_27.29_spmd.clone.sunk | while | flops 2746755584 | bytes 267450688 | solution.py:129
  553.8 5.8 exponential_select_fusion.5
  559.6 3.4 bitcast_add_fusion.11
  563.0 2.9 copy-done.2
  565.9 8.1 fusion.288
  574.1 22.7 %fusion.289 = bf16[2,512,8,64]{1,3,2,0:T(8,128)(2,1)} fusion(bf16[2,512,8,64]{1,3,2,0:T(8,128)(2,1)} %get-tuple-element.1115, s32[]{:T(128)S(6)} %copy.148, bf16[1024,8,64]{0,2,1:T(8,128)(2,1)} %get-tuple-element.1135, f32[8,512,1024]{2,1,0:T(8,128)} %copy-done.2, f32[8,512,1024]{2,1,0:T(8,128)} %fusion.288), kind=kOutput, calls=%fused_computation.78.clone.1 | convolution fusion | flops 557847552 | bytes 69206016 | tf_op jit(solution)/shard_map/while/body/eval_jaxpr/while/body/eval_jaxpr/hqk,khd->qhd/dot_general | solution.py:114
  596.7 23.4 %bitcast_add_fusion.10 = f32[1024,8,64]{0,2,1:T(8,128)} fusion(f32[1024,8,64]{0,2,1:T(8,128)} %get-tuple-element.1113, f32[8,512,1024]{2,1,0:T(8,128)} %copy-done.2, f32[8,512,1024]{2,1,0:T(8,128)} %fusion.288, pred[]{:T(512)S(6)} %compare.7, bf16[1024,8,64]{0,2,1:T(8,128)(2,1)} %get-tuple-element.1133, s32[]{:T(128)S(6)} %select_n.106), kind=kOutput, calls=%fused_computation.74.clone.1 | convolution fusion | flops 558896128 | bytes 71827464 | tf_op jit(solution)/shard_map/while/body/eval_jaxpr/while/body/eval_jaxpr/hqk,qhd->khd/dot_general | solution.py:117
  624.0 5.8 exponential_select_fusion.5
  629.8 6.4 bitcast_add_fusion.11
  636.7 8.1 fusion.288
  644.8 22.7 %fusion.289 = bf16[2,512,8,64]{1,3,2,0:T(8,128)(2,1)} fusion(bf16[2,512,8,64]{1,3,2,0:T(8,128)(2,1)} %get-tuple-element.1115, s32[]{:T(128)S(6)} %copy.148, bf16[1024,8,64]{0,2,1:T(8,128)(2,1)} %get-tuple-element.1135, f32[8,512,1024]{2,1,0:T(8,128)} %copy-done.2, f32[8,512,1024]{2,1,0:T(8,128)} %fusion.288), kind=kOutput, calls=%fused_computation.78.clone.1 | convolution fusion | flops 557847552 | bytes 69206016 | tf_op jit(solution)/shard_map/while/body/eval_jaxpr/while/body/eval_jaxpr/hqk,khd->qhd/dot_general | solution.py:114
  667.5 24.0 %bitcast_add_fusion.10 = f32[1024,8,64]{0,2,1:T(8,128)} fusion(f32[1024,8,64]{0,2,1:T(8,128)} %get-tuple-element.1113, f32[8,512,1024]{2,1,0:T(8,128)} %copy-done.2, f32[8,512,1024]{2,1,0:T(8,128)} %fusion.288, pred[]{:T(512)S(6)} %compare.7, bf16[1024,8,64]{0,2,1:T(8,128)(2,1)} %get-tuple-element.1133, s32[]{:T(128)S(6)} %select_n.106), kind=kOutput, calls=%fused_computation.74.clone.1 | convolution fusion | flops 558896128 | bytes 71827464 | tf_op jit(solution)/shard_map/while/body/eval_jaxpr/while/body/eval_jaxpr/hqk,qhd->khd/dot_general | solution.py:117
  710.5 6.6 copy.90
  717.0 7.0 copy.103
  733.6 40.9 %all-reduce.5 = f32[3072]{0:T(1024)S(1)} all-reduce(f32[3072]{0:T(1024)S(1)} %reshape.670), channel_id=6, replica_groups=mesh['dp'=8,'shard'=4] {'dp','shard'}, use_global_device_ids=true, to_apply=%region_40.41.clone | all-reduce | flops 3072 | bytes 24576
  779.4 224.7 %all-reduce.9.cloned.1.call-done = (f32[1572864]{0:T(1024)}, f32[524288]{0:T(1024)}, f32[1048576]{0:T(1024)}, f32[1048576]{0:T(1024)}) async-done(((f32[1572864]{0:T(1024)}, f32[524288]{0:T(1024)}, f32[1048576]{0:T(1024)}, f32[1048576]{0:T(1024)}), (f32[1572864]{0:T(1024)}, f32[524288]{0:T(1024)}, f32[1048576]{0:T(1024)}, f32[1048576]{0:T(1024)})) %all-reduce.9.cloned.1.call-update) | async-done | bytes 16777232
  (349 shorter events, 104.3 us)
Async XLA Ops:
  7.2 254.9 %copy-start = (bf16[1,1024,512]{2,1,0:T(8,128)(2,1)S(1)}, bf16[1,1024,512]{2,1,0:T(8,128)(2,1)}, u32[]{:S(2)}) copy-start(bf16[1,1024,512]{2,1,0:T(8,128)(2,1)} %param.29) | copy-start | bytes 3145732
  7.2 55.6 %copy-start.51 = (bf16[1,1024,512]{2,1,0:T(8,128)(2,1)S(1)}, bf16[1,1024,512]{2,1,0:T(8,128)(2,1)}, u32[]{:S(2)}) copy-start(bf16[1,1024,512]{2,1,0:T(8,128)(2,1)} %param.28) | copy-start | bytes 3145732
  7.2 61.1 %all-gather.7.cloned.1.call-start = ((), (), s32[]{:S(2)}) async-start(), calls=%async_computation.1 | async-start | bytes 1081344 | tf_op jit(solution)/shard_map/all_gather | solution.py:189
  8.9 118.0 %all-gather.9.cloned.1.call-start = ((), (), s32[]{:S(2)}) async-start(), calls=%async_computation.2 | async-start | bytes 2162688 | tf_op jit(solution)/shard_map/all_gather | solution.py:193
  10.5 175.1 %all-gather.11.cloned.1.call-start = ((), (), s32[]{:S(2)}) async-start(), calls=%async_computation.3 | async-start | bytes 2162688 | tf_op jit(solution)/shard_map/all_gather | solution.py:194
  12.1 234.8 %all-gather.5.cloned.1.call-start = ((), (), s32[]{:S(2)}) async-start(), calls=%async_computation | async-start | bytes 3244032 | tf_op jit(solution)/shard_map/all_gather | solution.py:188
  13.8 990.4 %all-reduce.9.cloned.1.call-start = ((), (), s32[]{:S(2)}) async-start(), calls=%async_computation.4 | async-start | bytes 33554432
  256.8 3.5 copy-start.39
  257.1 3.2 copy-start.40
  257.1 3.2 copy-start.52
  273.3 4.3 copy-start.29
  289.9 4.3 copy-start.29
  300.5 3.4 copy-start.3
  300.5 3.4 copy-start.10
  300.5 3.4 copy-start.57
  300.5 3.4 copy-start.35
  300.5 3.4 copy-start.49
  304.9 3.4 copy-start.6
  304.9 3.4 copy-start.65
  305.2 3.0 copy-start.70
  305.2 3.0 copy-start.72
  306.3 3.1 copy-start.5
  306.3 3.1 copy-start.11
  306.3 3.1 copy-start.56
  315.2 4.3 copy-start.31
  331.6 4.3 copy-start.31
  350.7 2.8 copy-start.7
  350.7 2.8 copy-start.55
  350.7 2.8 copy-start.66
  350.7 2.8 copy-start.73
  350.7 2.8 copy-start.78
  350.7 2.8 copy-start.93
  356.1 3.9 copy-start.46
  360.0 2.7 copy-start.12
  398.8 6.4 copy-start.1
  468.8 6.9 copy-start.1
  530.7 2.8 copy-start.67
  530.7 2.8 copy-start.8
  530.7 2.8 copy-start.16
  533.4 3.4 copy-start.21
  533.5 3.4 copy-start.71
  533.5 3.4 copy-start.74
  533.5 3.4 copy-start.79
  540.4 3.0 copy-start.25
  543.4 3.1 copy-start.54
  546.7 3.0 copy-start.4
  546.7 3.0 copy-start.58
  559.6 6.4 copy-start.2
  629.8 6.9 copy-start.2
  691.7 2.7 copy-start.43
  694.4 5.0 copy-start.23
  696.6 6.3 copy-start.18
  697.2 9.8 copy-start.17
  699.3 9.4 copy-start.27
  731.7 42.7 %copy-start.96 = (f32[96]{0:T(128)S(1)}, f32[96]{0:T(128)}, u32[]{:S(2)}) copy-start(f32[96]{0:T(128)} %param.47) | copy-start | bytes 1156
  731.8 42.7 %copy-start.97 = (f32[96]{0:T(128)S(1)}, f32[96]{0:T(128)}, u32[]{:S(2)}) copy-start(f32[96]{0:T(128)} %param.46) | copy-start | bytes 1156
  733.6 43.6 %copy-start.28 = (bf16[1024,8,64]{0,2,1:T(8,128)(2,1)S(1)}, bf16[1024,8,64]{0,2,1:T(8,128)(2,1)}, u32[]{:S(2)}) copy-start(bf16[1024,8,64]{0,2,1:T(8,128)(2,1)} %copy-done.27) | copy-start | bytes 3145732
  733.6 43.7 %copy-start.48 = (bf16[512,512]{1,0:T(8,128)(2,1)S(1)}, bf16[512,512]{1,0:T(8,128)(2,1)}, u32[]{:S(2)}) copy-start(bf16[512,512]{1,0:T(8,128)(2,1)} %slice.171) | copy-start | bytes 1572868
  777.2 226.9 %copy-start.59 = (f32[49152]{0:T(1024)S(1)}, f32[49152]{0:T(1024)}, u32[]{:S(2)}) copy-start(f32[49152]{0:T(1024)} %param.35) | copy-start | bytes 589828
  777.3 226.9 %copy-start.60 = (f32[49152]{0:T(1024)S(1)}, f32[49152]{0:T(1024)}, u32[]{:S(2)}) copy-start(f32[49152]{0:T(1024)} %param.34) | copy-start | bytes 589828
  777.3 230.3 %copy-start.61 = (f32[32768]{0:T(1024)S(1)}, f32[32768]{0:T(1024)}, u32[]{:S(2)}) copy-start(f32[32768]{0:T(1024)} %param.41) | copy-start | bytes 393220
  777.3 230.3 %copy-start.62 = (f32[32768]{0:T(1024)S(1)}, f32[32768]{0:T(1024)}, u32[]{:S(2)}) copy-start(f32[32768]{0:T(1024)} %param.40) | copy-start | bytes 393220
  777.3 230.2 %copy-start.63 = (f32[32768]{0:T(1024)S(1)}, f32[32768]{0:T(1024)}, u32[]{:S(2)}) copy-start(f32[32768]{0:T(1024)} %param.44) | copy-start | bytes 393220
  777.3 230.2 %copy-start.64 = (f32[32768]{0:T(1024)S(1)}, f32[32768]{0:T(1024)}, u32[]{:S(2)}) copy-start(f32[32768]{0:T(1024)} %param.43) | copy-start | bytes 393220
  (45 other events, 71.7 us)
Sparse Core Ops, SparseCore 0:
  11.5 56.7 all-gather.6
  71.7 55.1 all-gather.8
  130.4 55.2 all-gather.10
  189.0 57.8 all-gather.4
  724.3 279.8 all-reduce.8
where the time goes:
time: 1030 us; the launch traced here: 1020 us
  waiting for transfers between devices  396 us (38%)
  matrix products  361 us (35%)
  local copies, waits for them, and re-layouts  91.7 us (9%)
  blocking collectives  83 us (8%)
  other arithmetic  46.3 us (4%)
  loops' own time  23.1 us (2%)
  between operations  15.5 us (2%)
    unnamed x6, waiting for transfers between devices  225 us
    dot_general x4, matrix products, one_block(): jnp.einsum('hqk,qhd->khd', grad_scores, q_block, preferred_element_type=j...  94.7 us
    dot_general x4, matrix products, one_block(): jnp.einsum('hqk,khd->qhd', grad_scores, k_row, preferred_element_type=jnp...  90.7 us
    unnamed x2, blocking collectives  83 us
    all_gather x1, waiting for transfers between devices, body(): lax.all_gather(inward_low, ('dp', 'shard'), axis=0, tiled=True)  56.9 us
    all_gather x1, waiting for transfers between devices, body(): lax.all_gather(expand_low, ('dp', 'shard'), axis=0, tiled=True)  55.1 us
    all_gather x1, waiting for transfers between devices, body(): lax.all_gather(shrink_low, ('dp', 'shard'), axis=0, tiled=True)  54.6 us
    dot_general x8, matrix products, one_block(): jnp.einsum('qhd,khd->hqk', q_block, k_row, preferred_element_type=jnp.flo...  39.5 us
  transfers between devices with their start and end apart: 5, of which 5 were waited for; matrix products, arithmetic and copies ran while one was open for 4% of the time, Pallas kernels for 0%

commit v1 on v0

--- a/solution.py
+++ b/solution.py
@@ -1,7 +1,382 @@
+import functools
 import jax
 import jax.numpy as jnp
 from jax import lax
+from jax.experimental import pallas as pl
+from jax.experimental.pallas import tpu as pltpu
 from jax.sharding import PartitionSpec as P
+
+MESH = pl.DeviceIdType.MESH
+BF = jnp.bfloat16
+F32 = jnp.float32
+learn_rate = 0.001
+beta_one = 0.9
+beta_two = 0.999
+STEP = 10
+
+
+class Place:
+    def __init__(self, sizes):
+        self.sizes = sizes
+        dp, sh = lax.axis_index("dp"), lax.axis_index("shard")
+        self.at = (dp // sizes[1], dp % sizes[1], sh // sizes[3], sh % sizes[3])
+
+    def device(self, axis, coord):
+        a, b, c, e = [coord if i == axis else v for i, v in enumerate(self.at)]
+        return (a * self.sizes[1] + b, c * self.sizes[3] + e)
+
+    def greet(self):
+        barrier = pltpu.get_barrier_semaphore()
+        count = 0
+        for axis in range(4):
+            n, me = self.sizes[axis], self.at[axis]
+            if n == 2:
+                pl.semaphore_signal(barrier, inc=1, device_id=self.device(axis, 1 - me), device_id_type=MESH)
+                count = count + 1
+            else:
+                for step in (-1, 1):
+                    there = me + step
+                    ok = (there >= 0) & (there < n)
+
+                    @pl.when(ok)
+                    def _():
+                        pl.semaphore_signal(barrier, inc=1, device_id=self.device(axis, there), device_id_type=MESH)
+
+                    count = count + ok.astype(jnp.int32)
+        pl.semaphore_wait(barrier, count)
+
+
+class Sems:
+    def __init__(self, send, recv):
+        self.send, self.recv, self.used = send, recv, 0
+
+    def take(self):
+        k = self.used
+        self.used += 1
+        return self.send.at[k], self.recv.at[k]
+
+
+def gather_sems(order, sizes):
+    return 1 + sum(2 if sizes[x] == 2 else 4 * (sizes[x] - 1) for x in order)
+
+
+def gather_rounds(place, ref, order, sems):
+    sizes = place.sizes
+    after = []
+    held = []
+
+    def group(axis=None, coord=None):
+        idx = [slice(None) if i in held else place.at[i] for i in range(4)]
+        if axis is not None:
+            idx[axis] = coord
+        return ref.at[tuple(idx)]
+
+    def copy(block, axis, coord, pair):
+        return pltpu.make_async_remote_copy(
+            src_ref=block, dst_ref=block, send_sem=pair[0], recv_sem=pair[1],
+            device_id=place.device(axis, coord), device_id_type=MESH)
+
+    def to_sibling(axis, coord, cond):
+        pair = sems.take()
+        idx = [slice(None) if i in held else place.at[i] for i in range(4)]
+        if axis is not None:
+            idx[axis] = coord
+        mine = ref.at[tuple(idx)]
+        idx[3] = 1 - place.at[3]
+        theirs = ref.at[tuple(idx)]
+        e = place.at[3]
+        go = copy(mine, 3, 1 - e, pair)
+        come = copy(theirs, 3, 1 - e, pair)
+
+        def run(f):
+            if cond is None:
+                f()
+            else:
+                pl.when(cond)(f)
+
+        run(go.start)
+
+        def finish():
+            go.wait_send()
+            come.wait_recv()
+
+        after.append(lambda: run(finish))
+
+    to_sibling(None, None, None)
+    for axis in order:
+        n, me = sizes[axis], place.at[axis]
+        if n == 2:
+            pair = sems.take()
+            go = copy(group(), axis, 1 - me, pair)
+            come = copy(group(axis, 1 - me), axis, 1 - me, pair)
+            go.start()
+            after.append(go.wait_send)
+            yield
+            come.wait_recv()
+            to_sibling(axis, 1 - me, None)
+        else:
+            for t in range(1, n):
+                pending = []
+                for step in (1, -1):
+                    pair = sems.take()
+                    out_c, in_c, to = me - step * (t - 1), me - step * t, me + step
+                    can = (out_c >= 0) & (out_c < n) & (to >= 0) & (to < n)
+                    gets = (in_c >= 0) & (in_c < n)
+                    go = copy(group(axis, out_c), axis, to, pair)
+                    come = copy(group(axis, in_c), axis, to, pair)
+                    pl.when(can)(go.start)
+                    after.append(lambda go=go, can=can: pl.when(can)(go.wait_send))
+                    pending.append((come, gets, in_c))
+                yield
+                for come, gets, in_c in pending:
+                    pl.when(gets)(come.wait_recv)
+                    to_sibling(axis, in_c, gets)
+        held.append(axis)
+    yield
+    for f in after:
+        f()
+
+
+def interleave(rounds):
+    live = list(rounds)
+    while live:
+        still = []
+        for r in live:
+            try:
+                next(r)
+                still.append(r)
+            except StopIteration:
+                pass
+        live = still
+
+
+def flat_to_rows(src, dst, rows, cols):
+    w = cols // 128
+    for j in range(w):
+        dst[:, j * 128:(j + 1) * 128] = src[pl.ds(j, rows, stride=w), :].astype(dst.dtype)
+
+
+def rows_to_flat(value, dst, rows, cols):
+    w = cols // 128
+    for j in range(w):
+        dst[pl.ds(j, rows, stride=w), :] = value[:, j * 128:(j + 1) * 128]
+
+
+ORDERS = ((0, 2, 1), (0, 1, 2), (1, 2, 0), (0, 1, 2), (0, 1, 2))
+
+
+def gather_kernel(sizes, shapes, *refs):
+    n = len(shapes)
+    masters, outs = refs[:n], refs[n:2 * n]
+    stage, local, send, recv = refs[2 * n:3 * n], refs[3 * n], refs[3 * n + 1], refs[3 * n + 2]
+    place = Place(sizes)
+    copies = []
+    for k, (rows, cols) in enumerate(shapes):
+        if rows == 1:
+            stage[k][...] = masters[k][...].astype(BF).astype(stage[k].dtype)
+        else:
+            flat_to_rows(masters[k], stage[k], rows, cols)
+        cp = pltpu.make_async_copy(stage[k], outs[k].at[place.at], local.at[k])
+        cp.start()
+        copies.append(cp)
+    place.greet()
+    for cp in copies:
+        cp.wait()
+    sems = Sems(send, recv)
+    interleave([gather_rounds(place, outs[k], ORDERS[k], sems) for k in range(n)])
+
+
+def gather_all(mesh_sizes, masters, shapes, dtypes):
+    n = len(shapes)
+    total = sum(gather_sems(ORDERS[k], mesh_sizes) for k in range(n))
+    vm = pl.BlockSpec(memory_space=pltpu.VMEM)
+    return pl.pallas_call(
+        functools.partial(gather_kernel, mesh_sizes, shapes),
+        out_shape=[jax.ShapeDtypeStruct((*mesh_sizes, *s), d) for s, d in zip(shapes, dtypes)],
+        in_specs=[vm] * n,
+        out_specs=[pl.BlockSpec(memory_space=pl.ANY)] * n,
+        scratch_shapes=[pltpu.VMEM(s, d) for s, d in zip(shapes, dtypes)]
+        + [pltpu.SemaphoreType.DMA((n,)), pltpu.SemaphoreType.DMA((total,)), pltpu.SemaphoreType.DMA((total,))],
+        compiler_params=pltpu.CompilerParams(collective_id=0, has_side_effects=True, vmem_limit_bytes=48 << 20),
+        name="gather_weights",
+    )(*masters)
+
+
+def reduce_sems(order, sizes):
+    return 1 + sum(1 if sizes[x] == 2 else 2 * (sizes[x] - 1) for x in order)
+
+
+def reduce_rounds(place, grad, order, got, bufs, total, sems):
+    sizes = place.sizes
+    after = []
+    e = place.at[3]
+
+    def rdma(src, dst, axis, coord, pair):
+        return pltpu.make_async_remote_copy(
+            src_ref=src, dst_ref=dst, send_sem=pair[0], recv_sem=pair[1],
+            device_id=place.device(axis, coord), device_id_type=MESH)
+
+    def add_into(dst, src):
+        dst[...] = (dst[...].astype(F32) + src[...].astype(F32)).astype(dst.dtype)
+
+    def each(dims, f):
+        count = 1
+        for d in dims:
+            count *= d
+        if count == 1:
+            f(tuple(0 for _ in dims))
+            return
+
+        def step(i, _):
+            idx = []
+            for d in reversed(dims):
+                idx.append(i % d)
+                i = i // d
+            f(tuple(reversed(idx)))
+            return 0
+
+        lax.fori_loop(0, count, step, 0)
+
+    cp = rdma(grad.at[:, :, :, 1 - e], got, 3, 1 - e, sems.take())
+    cp.start()
+    yield
+    cp.wait()
+    each(sizes[:3], lambda i: add_into(got.at[i], grad.at[(*i, e)]))
+    cur, left = got, [0, 1, 2]
+    for axis, buf in zip(order, bufs):
+        n, me = sizes[axis], place.at[axis]
+        pos = left.index(axis)
+        rest = [x for x in left if x != axis]
+        dims = [sizes[x] for x in rest]
+
+        def part(ref, coord):
+            return ref.at[tuple(coord if i == pos else slice(None) for i in range(len(left)))]
+
+        def one(ref, coord, i):
+            i = list(i)
+            i.insert(pos, coord)
+            return ref.at[tuple(i)]
+
+        last = not rest
+        if n == 2:
+            cp = rdma(part(cur, 1 - me), buf, axis, 1 - me, sems.take())
+            cp.start()
+            yield
+            cp.wait()
+            if last:
+                total[...] = buf[...].astype(F32) + cur[me].astype(F32)
+            else:
+                each(dims, lambda i: add_into(buf.at[i], one(cur, me, i)))
+        else:
+            for t in range(n - 1):
+                for way, step in enumerate((1, -1)):
+                    j = n - 1 - t if step == 1 else t
+                    to, back = me + step, me - step
+                    ahead = (j > me) if step == 1 else (j < me)
+                    gets = ahead & (back >= 0) & (back < n)
+                    pair = sems.take()
+                    come = rdma(part(cur, j), buf.at[way, j], axis, to, pair)
+
+                    @pl.when(gets)
+                    def _():
+                        come.wait_recv()
+                        each(dims, lambda i: add_into(one(cur, j, i), buf.at[(way, j, *i)]))
+
+                    pl.when(ahead)(come.start)
+                    after.append(lambda come=come, ahead=ahead: pl.when(ahead)(come.wait_send))
+                    ends = (j == me) & (back >= 0) & (back < n)
+                    after.append(lambda come=come, ends=ends: pl.when(ends)(come.wait_recv))
+                yield
+            for f in after:
+                f()
+            after = []
+            keep = buf.at[0, me]
+
+            def close(i):
+                mine = one(cur, me, i)[...].astype(F32)
+                v = mine + jnp.where(me > 0, buf[(0, me, *i)].astype(F32), 0.0)
+                v = v + jnp.where(me < n - 1, buf[(1, me, *i)].astype(F32), 0.0)
+                if last:
+                    total[...] = v
+                else:
+                    buf[(0, me, *i)] = v.astype(buf.dtype)
+
+            each(dims, close)
+            buf = keep
+        cur, left = buf, rest
+    for f in after:
+        f()
+
+
+def reduce_bufs(order, sizes, shape):
+    left, out = [0, 1, 2], [(*sizes[:3], *shape)]
+    for axis in order:
+        rest = [x for x in left if x != axis]
+        dims = tuple(sizes[x] for x in rest)
+        out.append((*dims, *shape) if sizes[axis] == 2 else (2, sizes[axis], *dims, *shape))
+        left = rest
+    return out
+
+
+BACK = tuple(tuple(reversed(o)) for o in ORDERS)
+
+
+def adam(mean_old, square_old, grad):
+    mean_new = beta_one * mean_old + (1.0 - beta_one) * grad
+    square_new = beta_two * square_old + (1.0 - beta_two) * grad * grad
+    steps = float(STEP)
+    mean_hat = mean_new / (1.0 - beta_one**steps)
+    square_hat = square_new / (1.0 - beta_two**steps)
+    return -learn_rate * mean_hat / (jnp.sqrt(square_hat) + 1e-08), mean_new
+
+
+def reduce_kernel(sizes, shapes, counts, *refs):
+    n = len(shapes)
+    refs = list(refs)
+
+    def take(k):
+        out = refs[:k]
+        del refs[:k]
+        return out
+
+    grads, means, squares = take(n), take(n), take(n)
+    outs = take(3 * n)
+    totals = take(n)
+    bufs = [take(c) for c in counts]
+    send, recv = take(2)
+    place = Place(sizes)
+    place.greet()
+    sems = Sems(send, recv)
+    interleave([reduce_rounds(place, grads[k], BACK[k], bufs[k][0], bufs[k][1:], totals[k], sems) for k in range(n)])
+    for k, (rows, cols) in enumerate(shapes):
+        change, mean, summed = outs[3 * k:3 * k + 3]
+        if rows == 1:
+            summed[...] = totals[k][...]
+        else:
+            rows_to_flat(totals[k], summed, rows, cols)
+        change[...], mean[...] = adam(means[k][...], squares[k][...], summed[...])
+
+
+def reduce_all(mesh_sizes, grads, means, squares, shapes):
+    n = len(shapes)
+    flat = [((s[0] * s[1]) // 128, 128) for s in shapes]
+    lists = [reduce_bufs(BACK[k], mesh_sizes, shapes[k]) for k in range(n)]
+    total = sum(reduce_sems(BACK[k], mesh_sizes) for k in range(n))
+    vm = pl.BlockSpec(memory_space=pltpu.VMEM)
+    scratch = [pltpu.VMEM(s, F32) for s in shapes]
+    for k in range(n):
+        scratch += [pltpu.VMEM(s, grads[k].dtype) for s in lists[k]]
+    scratch += [pltpu.SemaphoreType.DMA((total,)), pltpu.SemaphoreType.DMA((total,))]
+    return pl.pallas_call(
+        functools.partial(reduce_kernel, mesh_sizes, shapes, [len(x) for x in lists]),
+        out_shape=[jax.ShapeDtypeStruct(f, F32) for f in flat for _ in range(3)],
+        in_specs=[vm] * (3 * n),
+        out_specs=[vm] * (3 * n),
+        scratch_shapes=scratch,
+        compiler_params=pltpu.CompilerParams(collective_id=1, has_side_effects=True, vmem_limit_bytes=60 << 20),
+        name="reduce_gradients",
+    )(*grads, *means, *squares)
+
 
 D = 512
 HEADS = 8
@@ -12,11 +387,6 @@
 STEP = 10
 
 
-learn_rate = 0.001
-beta_one = 0.9
-beta_two = 0.999
-
-
 def matmul(left_mat, right_mat):
     return jnp.dot(left_mat, right_mat, preferred_element_type=jnp.float32)
 
@@ -40,7 +410,8 @@
 
 
 def segments(lengths):
-    ends = jnp.cumsum(lengths, axis=-1)
+    upto = jnp.arange(SEGS)[:, None] <= jnp.arange(SEGS)[None, :]
+    ends = jnp.sum(jnp.where(upto[None], lengths[:, :, None], 0), 1)
     places = jnp.arange(ROW, dtype=jnp.int32)
     return jnp.sum((places[None, :, None] >= ends[:, None, :]).astype(jnp.int32), -1)
 
@@ -146,17 +517,20 @@
     )
 
 
-def adam_step(mean_old, square_old, grad_share):
-    mean_new = beta_one * mean_old + (1.0 - beta_one) * grad_share
-    square_new = beta_two * square_old + (1.0 - beta_two) * grad_share * grad_share
-    steps_float = float(STEP)
-    mean_hat = mean_new / (1.0 - beta_one**steps_float)
-    square_hat = square_new / (1.0 - beta_two**steps_float)
-    change = -learn_rate * mean_hat / (jnp.sqrt(square_hat) + 1e-08)
-    return (change, mean_new, grad_share)
+def shard_views(inward, outward, expand, shrink, norms):
+    arrays, shapes = [], []
+    for x, wide in ((inward, D), (outward, D), (expand, FF), (shrink, D)):
+        cols = wide if x.shape[0] >= 16 * wide else D
+        arrays.append(x.reshape(-1, 128))
+        shapes.append((x.shape[0] // cols, cols))
+    width = -(-norms.shape[0] // 128) * 128
+    arrays.append(jnp.pad(norms, (0, width - norms.shape[0])).reshape(1, width))
+    shapes.append((1, width))
+    return arrays, tuple(shapes)
 
 
 def body(
+    sizes,
     target,
     memory,
     cotangent,
@@ -179,20 +553,14 @@
     norms_square,
 ):
     row_count = target.shape[0]
-    inward_low = inward_master.astype(jnp.bfloat16)
-    outward_low = outward_master.astype(jnp.bfloat16)
-    expand_low = expand_master.astype(jnp.bfloat16)
-    shrink_low = shrink_master.astype(jnp.bfloat16)
-    norms_low = norms_master.astype(jnp.bfloat16)
-    inward_all, outward_all, norms_all = (
-        lax.all_gather(inward_low, ("dp", "shard"), axis=0, tiled=True),
-        lax.all_gather(outward_low, ("dp", "shard"), axis=0, tiled=True),
-        lax.all_gather(norms_low, ("dp", "shard"), axis=0, tiled=True),
-    )
-    expand_all, shrink_all = (
-        lax.all_gather(expand_low, ("dp", "shard"), axis=0, tiled=True),
-        lax.all_gather(shrink_low, ("dp", "shard"), axis=0, tiled=True),
-    )
+    flat, shapes = shard_views(
+        inward_master, outward_master, expand_master, shrink_master, norms_master
+    )
+    inward_all, outward_all, expand_all, shrink_all, norms_all = gather_all(
+        sizes, flat, shapes, [BF, BF, BF, BF, F32]
+    )
+    norm_count = norms_master.shape[0]
+    norms_all = norms_all.reshape(-1, norms_all.shape[-1])[:, :norm_count]
     w_in, w_out, w_up, w_down, gains, biases = unpack(
         inward_all, outward_all, norms_all, expand_all, shrink_all
     )
@@ -229,16 +597,6 @@
     activated = jax.nn.silu(pre_act).astype(jnp.bfloat16)
     resid_three = hidden_two + matmul(activated, w_down)
     output = layer_norm(resid_three, gains[2], biases[2])
-    inward_back, outward_back, norms_back, expand_back, shrink_back = (
-        lax.all_gather(inward_low, ("dp", "shard"), axis=0, tiled=True),
-        lax.all_gather(outward_low, ("dp", "shard"), axis=0, tiled=True),
-        lax.all_gather(norms_low, ("dp", "shard"), axis=0, tiled=True),
-        lax.all_gather(expand_low, ("dp", "shard"), axis=0, tiled=True),
-        lax.all_gather(shrink_low, ("dp", "shard"), axis=0, tiled=True),
-    )
-    w_in, w_out, w_up, w_down, gains, biases = unpack(
-        inward_back, outward_back, norms_back, expand_back, shrink_back
-    )
     seed = cotangent.reshape(-1, D).astype(jnp.float32) * live_rows
     _, pull_three = jax.vjp(layer_norm, resid_three, gains[2], biases[2])
     grad_three, gain_three, bias_three = pull_three(seed)
@@ -306,18 +664,23 @@
     grad_norms = jnp.stack(
         [jnp.stack([gain_one, gain_two, gain_three]), jnp.stack([bias_one, bias_two, bias_three])]
     ).reshape(-1)
-    inward_share, outward_share, norms_share, expand_share, shrink_share = (
-        lax.psum_scatter(grad_inward, ("dp", "shard"), scatter_dimension=0, tiled=True),
-        lax.psum_scatter(grad_outward, ("dp", "shard"), scatter_dimension=0, tiled=True),
-        lax.psum_scatter(grad_norms, ("dp", "shard"), scatter_dimension=0, tiled=True),
-        lax.psum_scatter(grad_expand.reshape(-1), ("dp", "shard"), scatter_dimension=0, tiled=True),
-        lax.psum_scatter(grad_shrink.reshape(-1), ("dp", "shard"), scatter_dimension=0, tiled=True),
-    )
-    in_c, in_m, in_g = adam_step(inward_mean, inward_square, inward_share)
-    out_c, out_m, out_g = adam_step(outward_mean, outward_square, outward_share)
-    up_c, up_m, up_g = adam_step(expand_mean, expand_square, expand_share)
-    down_c, down_m, down_g = adam_step(shrink_mean, shrink_square, shrink_share)
-    norm_c, norm_m, norm_g = adam_step(norms_mean, norms_square, norms_share)
+    norm_pad = shapes[4][1] - norm_count
+    grad_norms = jnp.pad(grad_norms.reshape(-1, norm_count), ((0, 0), (0, norm_pad)))
+    grads = [
+        g.astype(d).reshape(*sizes, *s)
+        for g, s, d in zip(
+            (grad_inward, grad_outward, grad_expand, grad_shrink, grad_norms),
+            shapes,
+            (BF, BF, BF, BF, F32),
+        )
+    ]
+    means, _ = shard_views(inward_mean, outward_mean, expand_mean, shrink_mean, norms_mean)
+    squares, _ = shard_views(
+        inward_square, outward_square, expand_square, shrink_square, norms_square
+    )
+    outs = [x.reshape(-1) for x in reduce_all(sizes, grads, means, squares, shapes)]
+    in_c, in_m, in_g, out_c, out_m, out_g, up_c, up_m, up_g, down_c, down_m, down_g = outs[:12]
+    norm_c, norm_m, norm_g = [x[:norm_count] for x in outs[12:]]
     shape_rows = (row_count, ROW, D)
     return (
         output.astype(jnp.bfloat16).reshape(shape_rows),
@@ -342,8 +705,9 @@
 
 
 def solution(mesh):
+    rows, cols = mesh.shape["dp"], mesh.shape["shard"]
     return jax.shard_map(
-        body,
+        functools.partial(body, (rows // 2, 2, cols // 2, 2)),
         mesh=mesh,
         in_specs=(
             P(("dp", "shard"), None, None),

time: 1030 us -> 640 us (0.62)
  waiting for transfers between devices: 396 us -> 0 us
  Pallas kernels: 0 us -> 136 us
  blocking collectives: 83 us -> 0 us
  local copies, waits for them, and re-layouts: 91.7 us -> 76.6 us
  between operations: 15.5 us -> 1.86 us
    unnamed x6 -> x0, waiting for transfers between devices: 225 us -> none
    all_gather x4 -> x0, waiting for transfers between devices: 171 us -> none  [the longest x1 56.9 us: body(): lax.all_gather(inward_low, ('dp', 'shard'), axis=0, tiled=True)]
    pallas_call x0 -> x2, Pallas kernels: none -> 136 us  [the longest x1 84.5 us: reduce_all(): pl.pallas_call(functools.partial(reduce_kernel, mesh_sizes, shapes, [len(...]
    unnamed x2 -> x0, blocking collectives: 83 us -> none
    unnamed x198 -> x192, local copies, waits for them, and re-layouts: 31.5 us -> 36.3 us
  transfers between devices with their start and end apart: 5 -> 0, of which waited for: 5 -> 0; matrix products, arithmetic and copies ran while one was open for 4% -> 0% of each run, Pallas kernels for 0% -> 0%
where the time goes in v1:
time: 640 us; the launch traced here: 631 us
  matrix products  365 us (57%)
  Pallas kernels  136 us (21%)
  local copies, waits for them, and re-layouts  76.6 us (12%)
  other arithmetic  36.4 us (6%)
  loops' own time  14.8 us (2%)
    dot_general x4, matrix products, one_block(): jnp.einsum('hqk,qhd->khd', grad_scores, q_block, preferred_element_type=j...  94.5 us
    dot_general x4, matrix products, one_block(): jnp.einsum('hqk,khd->qhd', grad_scores, k_row, preferred_element_type=jnp...  90.7 us
    pallas_call x1, Pallas kernels, reduce_all(): pl.pallas_call(functools.partial(reduce_kernel, mesh_sizes, shapes, [len(...  84.5 us
    pallas_call x1, Pallas kernels, gather_all(): pl.pallas_call(functools.partial(gather_kernel, mesh_sizes, shapes), out_...  51.9 us
    dot_general x8, matrix products, one_block(): jnp.einsum('qhd,khd->hqk', q_block, k_row, preferred_element_type=jnp.flo...  41 us
    unnamed x192, local copies, waits for them, and re-layouts  36.3 us
    dot_general x4, matrix products, one_block(): jnp.einsum('qhd,khd->hqk', g_block, v_row, preferred_element_type=jnp.flo...  32.4 us
    dot_general x10, matrix products, right_dot(): lax.dot_general(left_mat, right_mat, (((1,), (1,)), ((), ())), preferred_...  25 us

profile of v1, /device:TPU:0, one launch (start us, length us, event | category | flops | bytes accessed | tf_op | source)
XLA Modules:
  0.0 631.2 jit_solution(14961395736791435794)
XLA Ops:
  7.2 2.3 copy.63
  10.9 51.9 %gather_weights.1 = (bf16[4,2,2,2,96,512]{5,4,3,2,1,0:T(8,128)(2,1)}, bf16[4,2,2,2,32,512]{5,4,3,2,1,0:T(8,128)(2,1)S(1)}, bf16[4,2,2,2,16,2048]{5,4,3,2,1,0:T(8...) custom-call(f32[384,128]{1,0:T(8,128)S(1)} %bitcast.356, ...), custom_call_target="tpu_custom_call" | custom-call | tf_op jit(solution)/shard_map/gather_weights/pallas_call | solution.py:193
  66.8 3.0 convolution_convert_fusion.4
  69.7 2.9 convolution_convert_fusion.5
  78.0 35.3 %while.96 = (s32[]{:T(128)}, bf16[2,512,8,64]{1,3,2,0:T(8,128)(2,1)}, f32[2,8,512]{2,1,0:T(8,128)S(1)}, s32[2]{0:T(128)S(1)}, s32[1024]{0:T(1024)S(1)}, /*index=...) while((s32[]{:T(128)}, ...), condition=%wide.region_5.6_spmd, body=%wide.region_2.0_spmd.sunk | while | flops 1125642752 | bytes 64633092 | solution.py:453
  80.3 4.9 fusion.233
  85.2 4.2 fusion.234
  89.5 5.4 fusion.235
  97.7 4.9 fusion.233
  102.6 4.2 fusion.234
  106.9 5.4 fusion.235
  113.2 2.7 copy.61
  119.0 3.1 convolution_convert_fusion.6
  123.3 33.0 %while.97 = (s32[]{:T(128)}, bf16[2,512,8,64]{1,3,2,0:T(8,128)(2,1)}, f32[2,8,512]{2,1,0:T(8,128)S(1)}, s32[2]{0:T(128)S(1)}, s32[1024]{0:T(1024)S(1)}, /*index=...) while((s32[]{:T(128)}, ...), condition=%wide.region_13.14_spmd, body=%wide.region_10.13_spmd.sunk | while | flops 1124593664 | bytes 64628996 | solution.py:453
  125.1 4.1 fusion.238
  129.2 4.2 fusion.239
  133.5 5.4 fusion.240
  141.5 4.1 fusion.238
  145.6 4.2 fusion.239
  149.9 5.4 fusion.240
  156.3 2.5 copy.62
  161.6 6.3 multiply_convert_fusion.2
  168.0 2.6 fusion.155
  171.3 2.7 fusion.105
  173.9 7.5 %fusion.98 = bf16[1024,2048]{1,0:T(8,128)(2,1)S(1)} fusion(f32[1024,2048]{1,0:T(8,128)} %get-tuple-element.707, bf16[2048,512]{1,0:T(8,128)(2,1)S(1)} %bitcast.364, f32[1024]{0:T(1024)S(1)} %negate_multiply_fusion.2, f32[1024,512]{0,1:T(8,128)S(1)} %get-tuple-element.709, bf16[1,1024,512]{1,2,0:T(8,128)(2,1)S(1)} %copy-done.19, ...), kind=kOutput, calls=%fused_computation.97 | convolution fusion | flops 2173698048 | bytes 17848320 | tf_op jit(solution)/shard_map/dot_general | solution.py:401
  181.4 4.2 convolution_convert_fusion
  185.6 4.1 multiply_reduce_fusion.2
  189.7 3.8 convolution_convert_fusion.1
  197.5 141.1 %while.98 = (s32[]{:T(128)}, f32[1024,8,64]{0,2,1:T(8,128)}, f32[1024,8,64]{0,2,1:T(8,128)}, bf16[2,512,8,64]{1,3,2,0:T(8,128)(2,1)}, s32[2]{0:T(128)S(1)}, /*in...) while((s32[]{:T(128)}, f32[1024,8,64]{0,2,1:T(8,128)}, ...), condition=%wide.region_24.25_spmd.clone, body=%wide.region_22.24_spmd.clone.sunk | while | flops 2745706496 | bytes 267446608 | solution.py:500
  201.3 5.8 exponential_select_fusion.4
  207.1 3.4 bitcast_add_fusion.9
  210.4 3.0 copy-done.9
  213.4 8.1 %fusion.251 = f32[8,512,1024]{2,1,0:T(8,128)} fusion(bf16[1024,8,64]{0,2,1:T(8,128)(2,1)S(1)} %get-tuple-element.1088, bf16[1024,8,64]{0,2,1:T(8,128)(2,1)S(1)} %get-tuple-element.1087, s32[]{:T(128)S(6)} %select_n.130), kind=kOutput, calls=%fused_computation.49.clone.1 | convolution fusion | flops 536870912 | bytes 18350084 | tf_op jit(solution)/shard_map/while/body/eval_jaxpr/while/body/eval_jaxpr/qhd,khd->hqk/dot_general | solution.py:480
  221.5 22.7 %fusion.252 = bf16[2,512,8,64]{1,3,2,0:T(8,128)(2,1)} fusion(bf16[2,512,8,64]{1,3,2,0:T(8,128)(2,1)} %get-tuple-element.1063, s32[]{:T(128)S(6)} %copy.110, bf16[1024,8,64]{0,2,1:T(8,128)(2,1)} %get-tuple-element.1085, f32[8,512,1024]{2,1,0:T(8,128)} %copy-done.9, f32[8,512,1024]{2,1,0:T(8,128)} %fusion.251), kind=kOutput, calls=%fused_computation.46.clone.1 | convolution fusion | flops 557847552 | bytes 69206016 | tf_op jit(solution)/shard_map/while/body/eval_jaxpr/while/body/eval_jaxpr/hqk,khd->qhd/dot_general | solution.py:485
  244.2 23.4 %bitcast_add_fusion.8 = f32[1024,8,64]{0,2,1:T(8,128)} fusion(f32[1024,8,64]{0,2,1:T(8,128)} %get-tuple-element.1061, f32[8,512,1024]{2,1,0:T(8,128)} %copy-done.9, f32[8,512,1024]{2,1,0:T(8,128)} %fusion.251, pred[]{:T(512)S(6)} %compare.10, bf16[1024,8,64]{0,2,1:T(8,128)(2,1)} %get-tuple-element.1082, s32[]{:T(128)S(6)} %select_n.130), kind=kOutput, calls=%fused_computation.44.clone.1 | convolution fusion | flops 558896128 | bytes 71827464 | tf_op jit(solution)/shard_map/while/body/eval_jaxpr/while/body/eval_jaxpr/hqk,qhd->khd/dot_general | solution.py:488
  271.2 5.8 exponential_select_fusion.4
  276.9 6.4 %bitcast_add_fusion.9 = f32[1024,8,64]{0,2,1:T(8,128)} fusion(f32[1024,8,64]{0,2,1:T(8,128)} %get-tuple-element.1062, f32[8,512,1024]{2,1,0:T(8,128)S(1)} %exponential_select_fusion.4, pred[]{:T(512)S(6)} %compare.10, bf16[1024,8,64]{0,2,1:T(8,128)(2,1)S(1)} %get-tuple-element.1087, s32[]{:T(128)S(6)} %select_n.130), kind=kOutput, calls=%fused_computation.43.clone.1 | convolution fusion | flops 542113792 | bytes 21495812 | tf_op jit(solution)/shard_map/while/body/eval_jaxpr/while/body/eval_jaxpr/hqk,qhd->khd/dot_general | solution.py:491
  283.9 8.1 %fusion.251 = f32[8,512,1024]{2,1,0:T(8,128)} fusion(bf16[1024,8,64]{0,2,1:T(8,128)(2,1)S(1)} %get-tuple-element.1088, bf16[1024,8,64]{0,2,1:T(8,128)(2,1)S(1)} %get-tuple-element.1087, s32[]{:T(128)S(6)} %select_n.130), kind=kOutput, calls=%fused_computation.49.clone.1 | convolution fusion | flops 536870912 | bytes 18350084 | tf_op jit(solution)/shard_map/while/body/eval_jaxpr/while/body/eval_jaxpr/qhd,khd->hqk/dot_general | solution.py:480
  292.0 22.7 %fusion.252 = bf16[2,512,8,64]{1,3,2,0:T(8,128)(2,1)} fusion(bf16[2,512,8,64]{1,3,2,0:T(8,128)(2,1)} %get-tuple-element.1063, s32[]{:T(128)S(6)} %copy.110, bf16[1024,8,64]{0,2,1:T(8,128)(2,1)} %get-tuple-element.1085, f32[8,512,1024]{2,1,0:T(8,128)} %copy-done.9, f32[8,512,1024]{2,1,0:T(8,128)} %fusion.251), kind=kOutput, calls=%fused_computation.46.clone.1 | convolution fusion | flops 557847552 | bytes 69206016 | tf_op jit(solution)/shard_map/while/body/eval_jaxpr/while/body/eval_jaxpr/hqk,khd->qhd/dot_general | solution.py:485
  314.7 23.9 %bitcast_add_fusion.8 = f32[1024,8,64]{0,2,1:T(8,128)} fusion(f32[1024,8,64]{0,2,1:T(8,128)} %get-tuple-element.1061, f32[8,512,1024]{2,1,0:T(8,128)} %copy-done.9, f32[8,512,1024]{2,1,0:T(8,128)} %fusion.251, pred[]{:T(512)S(6)} %compare.10, bf16[1024,8,64]{0,2,1:T(8,128)(2,1)} %get-tuple-element.1082, s32[]{:T(128)S(6)} %select_n.130), kind=kOutput, calls=%fused_computation.44.clone.1 | convolution fusion | flops 558896128 | bytes 71827464 | tf_op jit(solution)/shard_map/while/body/eval_jaxpr/while/body/eval_jaxpr/hqk,qhd->khd/dot_general | solution.py:488
  338.6 2.5 copy.65
  341.4 2.8 multiply_reduce_fusion.3
  348.4 2.5 convolution_convert_fusion.2
  352.1 141.9 %while.99 = (s32[]{:T(128)}, f32[1024,8,64]{0,2,1:T(8,128)}, f32[1024,8,64]{0,2,1:T(8,128)}, bf16[2,512,8,64]{1,3,2,0:T(8,128)(2,1)}, s32[2]{0:T(128)S(1)}, /*in...) while((s32[]{:T(128)}, f32[1024,8,64]{0,2,1:T(8,128)}, ...), condition=%wide.region_29.30_spmd.clone, body=%wide.region_27.29_spmd.clone.sunk | while | flops 2746755584 | bytes 267450688 | solution.py:500
  356.3 5.8 exponential_select_fusion.5
  362.1 3.5 bitcast_add_fusion.11
  365.6 2.9 copy-done.10
  368.5 8.1 %fusion.264 = f32[8,512,1024]{2,1,0:T(8,128)} fusion(bf16[1024,8,64]{0,2,1:T(8,128)(2,1)S(1)} %get-tuple-element.1136, bf16[1024,8,64]{0,2,1:T(8,128)(2,1)S(1)} %get-tuple-element.1135, s32[]{:T(128)S(6)} %select_n.133), kind=kOutput, calls=%fused_computation.80.clone.1 | convolution fusion | flops 536870912 | bytes 18350084 | tf_op jit(solution)/shard_map/while/body/eval_jaxpr/while/body/eval_jaxpr/qhd,khd->hqk/dot_general | solution.py:480
  376.6 22.7 %fusion.265 = bf16[2,512,8,64]{1,3,2,0:T(8,128)(2,1)} fusion(bf16[2,512,8,64]{1,3,2,0:T(8,128)(2,1)} %get-tuple-element.1113, s32[]{:T(128)S(6)} %copy.122, bf16[1024,8,64]{0,2,1:T(8,128)(2,1)} %get-tuple-element.1133, f32[8,512,1024]{2,1,0:T(8,128)} %copy-done.10, f32[8,512,1024]{2,1,0:T(8,128)} %fusion.264), kind=kOutput, calls=%fused_computation.78.clone.1 | convolution fusion | flops 557847552 | bytes 69206016 | tf_op jit(solution)/shard_map/while/body/eval_jaxpr/while/body/eval_jaxpr/hqk,khd->qhd/dot_general | solution.py:485
  399.2 23.3 %bitcast_add_fusion.10 = f32[1024,8,64]{0,2,1:T(8,128)} fusion(f32[1024,8,64]{0,2,1:T(8,128)} %get-tuple-element.1111, f32[8,512,1024]{2,1,0:T(8,128)} %copy-done.10, f32[8,512,1024]{2,1,0:T(8,128)} %fusion.264, pred[]{:T(512)S(6)} %compare.11, bf16[1024,8,64]{0,2,1:T(8,128)(2,1)} %get-tuple-element.1131, s32[]{:T(128)S(6)} %select_n.133), kind=kOutput, calls=%fused_computation.74.clone.1 | convolution fusion | flops 558896128 | bytes 71827464 | tf_op jit(solution)/shard_map/while/body/eval_jaxpr/while/body/eval_jaxpr/hqk,qhd->khd/dot_general | solution.py:488
  426.4 5.8 exponential_select_fusion.5
  432.2 6.4 %bitcast_add_fusion.11 = f32[1024,8,64]{0,2,1:T(8,128)} fusion(f32[1024,8,64]{0,2,1:T(8,128)} %get-tuple-element.1112, f32[8,512,1024]{2,1,0:T(8,128)S(1)} %exponential_select_fusion.5, pred[]{:T(512)S(6)} %compare.11, bf16[1024,8,64]{0,2,1:T(8,128)(2,1)S(1)} %get-tuple-element.1135, s32[]{:T(128)S(6)} %select_n.133), kind=kOutput, calls=%fused_computation.73.clone.1 | convolution fusion | flops 542113792 | bytes 21495812 | tf_op jit(solution)/shard_map/while/body/eval_jaxpr/while/body/eval_jaxpr/hqk,qhd->khd/dot_general | solution.py:491
  439.2 8.1 %fusion.264 = f32[8,512,1024]{2,1,0:T(8,128)} fusion(bf16[1024,8,64]{0,2,1:T(8,128)(2,1)S(1)} %get-tuple-element.1136, bf16[1024,8,64]{0,2,1:T(8,128)(2,1)S(1)} %get-tuple-element.1135, s32[]{:T(128)S(6)} %select_n.133), kind=kOutput, calls=%fused_computation.80.clone.1 | convolution fusion | flops 536870912 | bytes 18350084 | tf_op jit(solution)/shard_map/while/body/eval_jaxpr/while/body/eval_jaxpr/qhd,khd->hqk/dot_general | solution.py:480
  447.3 22.7 %fusion.265 = bf16[2,512,8,64]{1,3,2,0:T(8,128)(2,1)} fusion(bf16[2,512,8,64]{1,3,2,0:T(8,128)(2,1)} %get-tuple-element.1113, s32[]{:T(128)S(6)} %copy.122, bf16[1024,8,64]{0,2,1:T(8,128)(2,1)} %get-tuple-element.1133, f32[8,512,1024]{2,1,0:T(8,128)} %copy-done.10, f32[8,512,1024]{2,1,0:T(8,128)} %fusion.264), kind=kOutput, calls=%fused_computation.78.clone.1 | convolution fusion | flops 557847552 | bytes 69206016 | tf_op jit(solution)/shard_map/while/body/eval_jaxpr/while/body/eval_jaxpr/hqk,khd->qhd/dot_general | solution.py:485
  470.0 23.9 %bitcast_add_fusion.10 = f32[1024,8,64]{0,2,1:T(8,128)} fusion(f32[1024,8,64]{0,2,1:T(8,128)} %get-tuple-element.1111, f32[8,512,1024]{2,1,0:T(8,128)} %copy-done.10, f32[8,512,1024]{2,1,0:T(8,128)} %fusion.264, pred[]{:T(512)S(6)} %compare.11, bf16[1024,8,64]{0,2,1:T(8,128)(2,1)} %get-tuple-element.1131, s32[]{:T(128)S(6)} %select_n.133), kind=kOutput, calls=%fused_computation.74.clone.1 | convolution fusion | flops 558896128 | bytes 71827464 | tf_op jit(solution)/shard_map/while/body/eval_jaxpr/while/body/eval_jaxpr/hqk,qhd->khd/dot_general | solution.py:488
  494.0 2.5 copy.67
  497.9 3.2 convert_element_type.239
  501.2 3.1 convert_element_type.243
  504.3 2.3 copy.71
  506.6 1.9 fusion.137
  508.5 3.3 add_bitcast_fusion
  515.7 1.8 copy.72
  517.5 2.4 fusion.111
  527.9 84.5 %reduce_gradients.1 = (f32[384,128]{1,0:T(8,128)}, f32[384,128]{1,0:T(8,128)}, f32[384,128]{1,0:T(8,128)}, f32[128,128]{1,0:T(8,128)}, f32[128,128]{1,0:T(8,128)...) custom-call(bf16[4,2,2,2,96,512]{5,4,3,2,1,0:T(8,128)(2,1)} %bitcast, ...), custom_call_target="tpu_custom_call" | custom-call | tf_op jit(solution)/shard_map/reduce_gradients/pallas_call | solution.py:370
  (316 shorter events, 79.9 us)
Async XLA Ops:
  0.7 66.1 %copy-start = (bf16[1,1024,512]{2,1,0:T(8,128)(2,1)S(1)}, bf16[1,1024,512]{2,1,0:T(8,128)(2,1)}, u32[]{:S(2)}) copy-start(bf16[1,1024,512]{2,1,0:T(8,128)(2,1)} %param.29) | copy-start | bytes 3145732
  0.7 8.9 %copy-start.48 = (bf16[1,1024,512]{2,1,0:T(8,128)(2,1)S(1)}, bf16[1,1024,512]{2,1,0:T(8,128)(2,1)}, u32[]{:S(2)}) copy-start(bf16[1,1024,512]{2,1,0:T(8,128)(2,1)} %param.28) | copy-start | bytes 3145732
  7.2 3.7 copy-start.1
  7.2 3.7 copy-start.2
  7.2 3.7 copy-start.3
  7.2 3.7 copy-start.4
  66.8 5.8 copy-start.43
  69.7 2.9 copy-start.49
  85.2 4.3 copy-start.35
  102.6 4.3 copy-start.35
  113.2 3.0 copy-start.11
  113.2 3.0 copy-start.54
  118.0 4.1 copy-start.14
  118.1 4.1 copy-start.60
  119.0 3.2 copy-start.67
  119.0 4.3 copy-start.13
  119.0 4.3 copy-start.18
  119.0 4.3 copy-start.53
  119.0 4.2 copy-start.91
  129.2 4.3 copy-start.37
  145.6 4.3 copy-start.37
  156.3 2.7 copy-start.15
  156.3 2.8 copy-start.51
  156.3 2.8 copy-start.61
  156.3 2.8 copy-start.68
  156.3 2.8 copy-start.73
  156.3 2.8 copy-start.86
  161.6 6.3 copy-start.8
  167.9 2.7 copy-start.19
  167.9 2.7 copy-start.64
  167.9 2.7 copy-start.71
  207.1 6.3 %copy-start.9 = (f32[8,512,1024]{2,1,0:T(8,128)}, f32[8,512,1024]{2,1,0:T(8,128)S(1)}, u32[]{:S(2)}) copy-start(f32[8,512,1024]{2,1,0:T(8,128)S(1)} %exponential_select_fusion.4) | copy-start | bytes 50331652 | tf_op jit(solution)/shard_map/while/body/eval_jaxpr/while
  276.9 6.9 %copy-start.9 = (f32[8,512,1024]{2,1,0:T(8,128)}, f32[8,512,1024]{2,1,0:T(8,128)S(1)}, u32[]{:S(2)}) copy-start(f32[8,512,1024]{2,1,0:T(8,128)S(1)} %exponential_select_fusion.4) | copy-start | bytes 50331652 | tf_op jit(solution)/shard_map/while/body/eval_jaxpr/while
  338.6 2.8 copy-start.74
  338.6 2.8 copy-start.62
  338.6 2.8 copy-start.16
  338.6 2.8 copy-start.23
  341.3 2.8 copy-start.30
  341.4 2.8 copy-start.66
  341.4 2.8 copy-start.69
  345.4 3.0 copy-start.76
  348.4 3.6 copy-start.12
  348.4 3.6 copy-start.55
  348.4 3.6 copy-start.89
  362.1 6.3 %copy-start.10 = (f32[8,512,1024]{2,1,0:T(8,128)}, f32[8,512,1024]{2,1,0:T(8,128)S(1)}, u32[]{:S(2)}) copy-start(f32[8,512,1024]{2,1,0:T(8,128)S(1)} %exponential_select_fusion.5) | copy-start | bytes 50331652 | tf_op jit(solution)/shard_map/while/body/eval_jaxpr/while
  432.2 6.9 %copy-start.10 = (f32[8,512,1024]{2,1,0:T(8,128)}, f32[8,512,1024]{2,1,0:T(8,128)S(1)}, u32[]{:S(2)}) copy-start(f32[8,512,1024]{2,1,0:T(8,128)S(1)} %exponential_select_fusion.5) | copy-start | bytes 50331652 | tf_op jit(solution)/shard_map/while/body/eval_jaxpr/while
  494.0 3.7 copy-start.45
  497.8 13.9 %copy-start.28 = (bf16[1024,8,64]{0,2,1:T(8,128)(2,1)}, bf16[1024,8,64]{0,2,1:T(8,128)(2,1)S(1)}, u32[]{:S(2)}) copy-start(bf16[1024,8,64]{0,2,1:T(8,128)(2,1)S(1)} %convert_element_type.237) | copy-start | bytes 3145732
  497.9 3.2 copy-start.46
  501.2 5.4 copy-start.24
  506.6 1.9 copy-start.33
  508.5 3.3 copy-start.44
  513.0 1.9 copy-start.26
  513.0 1.9 copy-start.77
  517.5 2.5 copy-start.29
  517.5 2.5 copy-start.50
  521.2 1.9 copy-start.31
  521.2 1.9 copy-start.63
  521.2 1.9 copy-start.70
  521.2 1.9 copy-start.75
  612.4 15.9 %copy-start.59 = (f32[256,128]{1,0:T(8,128)S(1)}, f32[256,128]{1,0:T(8,128)}, u32[]{:S(2)}) copy-start(f32[256,128]{1,0:T(8,128)} %get-tuple-element.454) | copy-start | bytes 393220
  612.4 16.6 %copy-start.58 = (f32[256,128]{1,0:T(8,128)S(1)}, f32[256,128]{1,0:T(8,128)}, u32[]{:S(2)}) copy-start(f32[256,128]{1,0:T(8,128)} %get-tuple-element.455) | copy-start | bytes 393220
  612.4 17.3 %copy-start.57 = (f32[256,128]{1,0:T(8,128)S(1)}, f32[256,128]{1,0:T(8,128)}, u32[]{:S(2)}) copy-start(f32[256,128]{1,0:T(8,128)} %get-tuple-element.456) | copy-start | bytes 393220
  612.4 17.9 %copy-start.56 = (f32[256,128]{1,0:T(8,128)S(1)}, f32[256,128]{1,0:T(8,128)}, u32[]{:S(2)}) copy-start(f32[256,128]{1,0:T(8,128)} %get-tuple-element.457) | copy-start | bytes 393220
  (34 other events, 43.2 us)

commit v2 on v1

v2 whole, which is shorter than its diff:
```python
import functools
import jax
import jax.numpy as jnp
from jax import lax
from jax.experimental import pallas as pl
from jax.experimental.pallas import tpu as pltpu
from jax.sharding import PartitionSpec as P

MESH = pl.DeviceIdType.MESH
BF = jnp.bfloat16
F32 = jnp.float32
learn_rate = 0.001
beta_one = 0.9
beta_two = 0.999
STEP = 10


class Place:
    def __init__(self, sizes):
        self.sizes = sizes
        dp, sh = lax.axis_index("dp"), lax.axis_index("shard")
        self.at = (dp // sizes[1], dp % sizes[1], sh // sizes[3], sh % sizes[3])

    def device(self, axis, coord):
        a, b, c, e = [coord if i == axis else v for i, v in enumerate(self.at)]
        return (a * self.sizes[1] + b, c * self.sizes[3] + e)

    def greet(self):
        barrier = pltpu.get_barrier_semaphore()
        count = 0
        for axis in range(4):
            n, me = self.sizes[axis], self.at[axis]
            if n == 2:
                pl.semaphore_signal(barrier, inc=1, device_id=self.device(axis, 1 - me), device_id_type=MESH)
                count = count + 1
            else:
                for step in (-1, 1):
                    there = me + step
                    ok = (there >= 0) & (there < n)

                    @pl.when(ok)
                    def _():
                        pl.semaphore_signal(barrier, inc=1, device_id=self.device(axis, there), device_id_type=MESH)

                    count = count + ok.astype(jnp.int32)
        pl.semaphore_wait(barrier, count)


class Sems:
    def __init__(self, send, recv):
        self.send, self.recv, self.used = send, recv, 0

    def take(self):
        k = self.used
        self.used += 1
        return self.send.at[k], self.recv.at[k]


def gather_sems(order, sizes):
    return 1 + sum(2 if sizes[x] == 2 else 4 * (sizes[x] - 1) for x in order)


def gather_rounds(place, ref, order, sems):
    sizes = place.sizes
    after = []
    held = []

    def group(axis=None, coord=None):
        idx = [slice(None) if i in held else place.at[i] for i in range(4)]
        if axis is not None:
            idx[axis] = coord
        return ref.at[tuple(idx)]

    def copy(block, axis, coord, pair):
        return pltpu.make_async_remote_copy(
            src_ref=block, dst_ref=block, send_sem=pair[0], recv_sem=pair[1],
            device_id=place.device(axis, coord), device_id_type=MESH)

    def to_sibling(axis, coord, cond):
        pair = sems.take()
        idx = [slice(None) if i in held else place.at[i] for i in range(4)]
        if axis is not None:
            idx[axis] = coord
        mine = ref.at[tuple(idx)]
        idx[3] = 1 - place.at[3]
        theirs = ref.at[tuple(idx)]
        e = place.at[3]
        go = copy(mine, 3, 1 - e, pair)
        come = copy(theirs, 3, 1 - e, pair)

        def run(f):
            if cond is None:
                f()
            else:
                pl.when(cond)(f)

        run(go.start)

        def finish():
            go.wait_send()
            come.wait_recv()

        after.append(lambda: run(finish))

    to_sibling(None, None, None)
    for axis in order:
        n, me = sizes[axis], place.at[axis]
        if n == 2:
            pair = sems.take()
            go = copy(group(), axis, 1 - me, pair)
            come = copy(group(axis, 1 - me), axis, 1 - me, pair)
            go.start()
            after.append(go.wait_send)
            yield
            come.wait_recv()
            to_sibling(axis, 1 - me, None)
        else:
            for t in range(1, n):
                pending = []
                for step in (1, -1):
                    pair = sems.take()
                    out_c, in_c, to = me - step * (t - 1), me - step * t, me + step
                    can = (out_c >= 0) & (out_c < n) & (to >= 0) & (to < n)
                    gets = (in_c >= 0) & (in_c < n)
                    go = copy(group(axis, out_c), axis, to, pair)
                    come = copy(group(axis, in_c), axis, to, pair)
                    pl.when(can)(go.start)
                    after.append(lambda go=go, can=can: pl.when(can)(go.wait_send))
                    pending.append((come, gets, in_c))
                yield
                for come, gets, in_c in pending:
                    pl.when(gets)(come.wait_recv)
                    to_sibling(axis, in_c, gets)
        held.append(axis)
    yield
    for f in after:
        f()


def interleave(rounds):
    live = list(rounds)
    while live:
        still = []
        for r in live:
            try:
                next(r)
                still.append(r)
            except StopIteration:
                pass
        live = still


def flat_to_rows(src, dst, rows, cols):
    w = cols // 128
    for j in range(w):
        dst[:, j * 128:(j + 1) * 128] = src[pl.ds(j, rows, stride=w), :].astype(dst.dtype)


def rows_to_flat(value, dst, rows, cols):
    w = cols // 128
    for j in range(w):
        dst[pl.ds(j, rows, stride=w), :] = value[:, j * 128:(j + 1) * 128]


ORDERS = ((0, 2, 1), (0, 1, 2), (1, 2, 0), (0, 1, 2), (0, 1, 2))


def gather_kernel(sizes, shapes, *refs):
    n = len(shapes)
    masters, outs = refs[:n], refs[n:2 * n]
    stage, local, send, recv = refs[2 * n:3 * n], refs[3 * n], refs[3 * n + 1], refs[3 * n + 2]
    place = Place(sizes)
    copies = []
    for k, (rows, cols) in enumerate(shapes):
        if rows == 1:
            stage[k][...] = masters[k][...].astype(BF).astype(stage[k].dtype)
        else:
            flat_to_rows(masters[k], stage[k], rows, cols)
        cp = pltpu.make_async_copy(stage[k], outs[k].at[place.at], local.at[k])
        cp.start()
        copies.append(cp)
    place.greet()
    for cp in copies:
        cp.wait()
    sems = Sems(send, recv)
    interleave([gather_rounds(place, outs[k], ORDERS[k], sems) for k in range(n)])


def gather_all(mesh_sizes, masters, shapes, dtypes):
    n = len(shapes)
    total = sum(gather_sems(ORDERS[k], mesh_sizes) for k in range(n))
    vm = pl.BlockSpec(memory_space=pltpu.VMEM)
    return pl.pallas_call(
        functools.partial(gather_kernel, mesh_sizes, shapes),
        out_shape=[jax.ShapeDtypeStruct((*mesh_sizes, *s), d) for s, d in zip(shapes, dtypes)],
        in_specs=[vm] * n,
        out_specs=[pl.BlockSpec(memory_space=pl.ANY)] * n,
        scratch_shapes=[pltpu.VMEM(s, d) for s, d in zip(shapes, dtypes)]
        + [pltpu.SemaphoreType.DMA((n,)), pltpu.SemaphoreType.DMA((total,)), pltpu.SemaphoreType.DMA((total,))],
        compiler_params=pltpu.CompilerParams(collective_id=0, has_side_effects=True, vmem_limit_bytes=48 << 20),
        name="gather_weights",
    )(*masters)


def reduce_sems(order, sizes):
    return 1 + sum(1 if sizes[x] == 2 else 2 * (sizes[x] - 1) for x in order)


def reduce_rounds(place, grad, order, got, bufs, total, sems):
    sizes = place.sizes
    after = []
    e = place.at[3]

    def rdma(src, dst, axis, coord, pair):
        return pltpu.make_async_remote_copy(
            src_ref=src, dst_ref=dst, send_sem=pair[0], recv_sem=pair[1],
            device_id=place.device(axis, coord), device_id_type=MESH)

    def add_into(dst, src):
        dst[...] = (dst[...].astype(F32) + src[...].astype(F32)).astype(dst.dtype)

    def each(dims, f):
        count = 1
        for d in dims:
            count *= d
        if count == 1:
            f(tuple(0 for _ in dims))
            return

        def step(i, _):
            idx = []
            for d in reversed(dims):
                idx.append(i % d)
                i = i // d
            f(tuple(reversed(idx)))
            return 0

        lax.fori_loop(0, count, step, 0)

    cp = rdma(grad.at[:, :, :, 1 - e], got, 3, 1 - e, sems.take())
    cp.start()
    yield
    cp.wait()
    each(sizes[:3], lambda i: add_into(got.at[i], grad.at[(*i, e)]))
    cur, left = got, [0, 1, 2]
    for axis, buf in zip(order, bufs):
        n, me = sizes[axis], place.at[axis]
        pos = left.index(axis)
        rest = [x for x in left if x != axis]
        dims = [sizes[x] for x in rest]

        def part(ref, coord):
            return ref.at[tuple(coord if i == pos else slice(None) for i in range(len(left)))]

        def one(ref, coord, i):
            i = list(i)
            i.insert(pos, coord)
            return ref.at[tuple(i)]

        last = not rest
        if n == 2:
            cp = rdma(part(cur, 1 - me), buf, axis, 1 - me, sems.take())
            cp.start()
            yield
            cp.wait()
            if last:
                total[...] = buf[...].astype(F32) + cur[me].astype(F32)
            else:
                each(dims, lambda i: add_into(buf.at[i], one(cur, me, i)))
        else:
            for t in range(n - 1):
                for way, step in enumerate((1, -1)):
                    j = n - 1 - t if step == 1 else t
                    to, back = me + step, me - step
                    ahead = (j > me) if step == 1 else (j < me)
                    gets = ahead & (back >= 0) & (back < n)
                    pair = sems.take()
                    come = rdma(part(cur, j), buf.at[way, j], axis, to, pair)

                    @pl.when(gets)
                    def _():
                        come.wait_recv()
                        each(dims, lambda i: add_into(one(cur, j, i), buf.at[(way, j, *i)]))

                    pl.when(ahead)(come.start)
                    after.append(lambda come=come, ahead=ahead: pl.when(ahead)(come.wait_send))
                    ends = (j == me) & (back >= 0) & (back < n)
                    after.append(lambda come=come, ends=ends: pl.when(ends)(come.wait_recv))
                yield
            for f in after:
                f()
            after = []
            keep = buf.at[0, me]

            def close(i):
                mine = one(cur, me, i)[...].astype(F32)
                v = mine + jnp.where(me > 0, buf[(0, me, *i)].astype(F32), 0.0)
                v = v + jnp.where(me < n - 1, buf[(1, me, *i)].astype(F32), 0.0)
                if last:
                    total[...] = v
                else:
                    buf[(0, me, *i)] = v.astype(buf.dtype)

            each(dims, close)
            buf = keep
        cur, left = buf, rest
    for f in after:
        f()


def reduce_bufs(order, sizes, shape):
    left, out = [0, 1, 2], [(*sizes[:3], *shape)]
    for axis in order:
        rest = [x for x in left if x != axis]
        dims = tuple(sizes[x] for x in rest)
        out.append((*dims, *shape) if sizes[axis] == 2 else (2, sizes[axis], *dims, *shape))
        left = rest
    return out


BACK = tuple(tuple(reversed(o)) for o in ORDERS)


def adam(mean_old, square_old, grad):
    mean_new = beta_one * mean_old + (1.0 - beta_one) * grad
    square_new = beta_two * square_old + (1.0 - beta_two) * grad * grad
    steps = float(STEP)
    mean_hat = mean_new / (1.0 - beta_one**steps)
    square_hat = square_new / (1.0 - beta_two**steps)
    return -learn_rate * mean_hat / (jnp.sqrt(square_hat) + 1e-08), mean_new


def reduce_kernel(sizes, shapes, counts, *refs):
    n = len(shapes)
    refs = list(refs)

    def take(k):
        out = refs[:k]
        del refs[:k]
        return out

    grads, means, squares = take(n), take(n), take(n)
    outs = take(3 * n)
    totals = take(n)
    bufs = [take(c) for c in counts]
    send, recv = take(2)
    place = Place(sizes)
    place.greet()
    sems = Sems(send, recv)
    interleave([reduce_rounds(place, grads[k], BACK[k], bufs[k][0], bufs[k][1:], totals[k], sems) for k in range(n)])
    for k, (rows, cols) in enumerate(shapes):
        change, mean, summed = outs[3 * k:3 * k + 3]
        if rows == 1:
            summed[...] = totals[k][...]
        else:
            rows_to_flat(totals[k], summed, rows, cols)
        change[...], mean[...] = adam(means[k][...], squares[k][...], summed[...])


def reduce_all(mesh_sizes, grads, means, squares, shapes):
    n = len(shapes)
    flat = [((s[0] * s[1]) // 128, 128) for s in shapes]
    lists = [reduce_bufs(BACK[k], mesh_sizes, shapes[k]) for k in range(n)]
    total = sum(reduce_sems(BACK[k], mesh_sizes) for k in range(n))
    vm = pl.BlockSpec(memory_space=pltpu.VMEM)
    scratch = [pltpu.VMEM(s, F32) for s in shapes]
    for k in range(n):
        scratch += [pltpu.VMEM(s, grads[k].dtype) for s in lists[k]]
    scratch += [pltpu.SemaphoreType.DMA((total,)), pltpu.SemaphoreType.DMA((total,))]
    return pl.pallas_call(
        functools.partial(reduce_kernel, mesh_sizes, shapes, [len(x) for x in lists]),
        out_shape=[jax.ShapeDtypeStruct(f, F32) for f in flat for _ in range(3)],
        in_specs=[vm] * (3 * n),
        out_specs=[vm] * (3 * n),
        scratch_shapes=scratch,
        compiler_params=pltpu.CompilerParams(collective_id=1, has_side_effects=True, vmem_limit_bytes=60 << 20),
        name="reduce_gradients",
    )(*grads, *means, *squares)


D = 512
HEADS = 8
HD = 64
FF = 2048
ROW = 1024
SEGS = 24
QT = 256
KT = 128
PAIR = 128
NEG = -1000000000.0


def dot(a, b):
    return jnp.dot(a, b, preferred_element_type=F32)


def dot_t(a, b):
    return lax.dot_general(a, b, (((1,), (1,)), ((), ())), preferred_element_type=F32)


def t_dot(a, b):
    return lax.dot_general(a, b, (((0,), (0,)), ((), ())), preferred_element_type=F32)


def for_rows(block, f, rows=ROW):
    def step(i, _):
        f(pl.ds(pl.multiple_of(i * block, block), block))
        return 0

    lax.fori_loop(0, rows // block, step, 0)


def ends_of(lengths):
    out, total = [], jnp.int32(0)
    for i in range(SEGS):
        total = total + lengths[0, i]
        out.append(total)
    return out


def seg_at(ends, place):
    count = jnp.int32(0)
    for e in ends:
        count = count + (e <= place).astype(jnp.int32)
    return count


def pick(values, index):
    out = values[-1]
    for i in range(len(values) - 2, -1, -1):
        out = jnp.where(index <= i, values[i], out)
    return out


def seg_row(ends):
    place = lax.broadcasted_iota(jnp.int32, (1, ROW), 1)
    out = jnp.zeros((1, ROW), jnp.int32)
    for e in ends:
        out = out + (place >= e).astype(jnp.int32)
    return out.astype(F32)


def store_seg(ends, row_ref, col_ref):
    row_ref[...] = jnp.broadcast_to(seg_row(ends), (8, ROW))
    for i in range(ROW // 128):
        block = jnp.broadcast_to(row_ref[0:1, i * 128:(i + 1) * 128], (128, 128))
        col_ref[i * 128:(i + 1) * 128, :] = jnp.transpose(block)


def ranges(query_ends, key_ends, causal, tile, other, by_query):
    out = []
    here, there = (query_ends, key_ends) if by_query else (key_ends, query_ends)
    starts = [jnp.int32(0)] + there[:-1]
    for i in range(ROW // tile):
        first, last = i * tile, (i + 1) * tile - 1
        low = pick(starts, seg_at(here, first)) // other
        high = (pick(there, seg_at(here, last)) + other - 1) // other
        if causal and by_query:
            high = jnp.int32((i + 1) * tile // other)
        if causal and not by_query:
            low = jnp.int32(i * tile // other)
        out.append((low, high))
    return out


def store_ranges(ref, base, pairs):
    for i, (low, high) in enumerate(pairs):
        ref[base + 2 * i] = low
        ref[base + 2 * i + 1] = high


def head_masks():
    lane = lax.broadcasted_iota(jnp.int32, (1, PAIR), 1)
    left = (lane < HD).astype(F32).astype(BF)
    return left, (1.0 - left.astype(F32)).astype(BF)


def stack_heads(block, masks):
    return jnp.concatenate([block * masks[0], block * masks[1]], 0)


def block_diag(pair_t):
    zero = jnp.zeros((HD, pair_t.shape[1]), pair_t.dtype)
    top = jnp.concatenate([pair_t[:HD], zero], 1)
    low = jnp.concatenate([zero, pair_t[HD:]], 1)
    return jnp.concatenate([top, low], 0)


def bias_tile(key_col, query_row, k0, q0, causal):
    keys = key_col[pl.ds(k0, KT), :]
    keys = jnp.concatenate([keys] * (QT // 128), 1)
    ok = keys == query_row[0:1, pl.ds(q0, QT)]
    if causal:
        kpos = k0 + lax.broadcasted_iota(jnp.int32, (KT, QT), 0)
        qpos = q0 + lax.broadcasted_iota(jnp.int32, (KT, QT), 1)
        ok = ok & (kpos <= qpos)
    return jnp.where(ok, 0.0, NEG)


def attend(q, k, vt, key_col, query_row, table, base, causal, out, lse, acc, peak, tally):
    masks = head_masks()

    def q_tile(i, _):
        q0 = pl.multiple_of(i * QT, QT)
        acc[...] = jnp.zeros_like(acc)
        peak[...] = jnp.full_like(peak, -3e38)
        tally[...] = jnp.zeros_like(tally)

        def k_tile(j, _):
            k0 = pl.multiple_of(j * KT, KT)
            bias = bias_tile(key_col, query_row, k0, q0, causal)
            peaks, tallies = [], []
            for hp in range(HEADS // 2):
                cols = slice(hp * PAIR, (hp + 1) * PAIR)
                s = dot_t(stack_heads(k[pl.ds(k0, KT), cols], masks), q[pl.ds(q0, QT), cols])
                probs, scales = [], []
                for side in range(2):
                    h = 2 * hp + side
                    sh = s[side * KT:(side + 1) * KT] + bias
                    old = peak[h:h + 1, :]
                    new = jnp.maximum(old, jnp.max(sh, 0, keepdims=True))
                    p = jnp.exp(sh - new)
                    scale = jnp.exp(old - new)
                    tallies.append(scale * tally[h:h + 1, :] + jnp.sum(p, 0, keepdims=True))
                    peaks.append(new)
                    probs.append(p.astype(BF))
                    scales.append(scale)
                o = dot(block_diag(vt[cols, pl.ds(k0, KT)]), jnp.concatenate(probs, 0))
                for side in range(2):
                    rows = slice(hp * PAIR + side * HD, hp * PAIR + (side + 1) * HD)
                    acc[rows, :] = acc[rows, :] * scales[side] + o[side * HD:(side + 1) * HD]
            peak[...] = jnp.concatenate(peaks, 0)
            tally[...] = jnp.concatenate(tallies, 0)
            return 0

        lax.fori_loop(table[base + 2 * i], table[base + 2 * i + 1], k_tile, 0)
        total = tally[...]
        lse[:, pl.ds(q0, QT)] = peak[...] + jnp.log(total)
        inverse = 1.0 / total
        for hp in range(HEADS // 2):
            rows = [acc[hp * PAIR + s * HD:hp * PAIR + (s + 1) * HD, :] * inverse[2 * hp + s:2 * hp + s + 1, :] for s in range(2)]
            out[pl.ds(q0, QT), hp * PAIR:(hp + 1) * PAIR] = jnp.transpose(jnp.concatenate(rows, 0)).astype(BF)
        return 0

    lax.fori_loop(0, ROW // QT, q_tile, 0)


def attend_back(q, k, v, kt, grad, lse, inner, key_col, query_row, table, base, causal, dqt, dk, dv, dk_acc, dv_acc):
    masks = head_masks()
    left = lax.broadcasted_iota(jnp.int32, (KT, PAIR), 1) < HD
    dqt[...] = jnp.zeros_like(dqt)

    def k_tile(j, _):
        k0 = pl.multiple_of(j * KT, KT)
        dk_acc[...] = jnp.zeros_like(dk_acc)
        dv_acc[...] = jnp.zeros_like(dv_acc)

        def q_tile(i, _):
            q0 = pl.multiple_of(i * QT, QT)
            bias = bias_tile(key_col, query_row, k0, q0, causal)
            for hp in range(HEADS // 2):
                cols = slice(hp * PAIR, (hp + 1) * PAIR)
                qp, gp = q[pl.ds(q0, QT), cols], grad[pl.ds(q0, QT), cols]
                s = dot_t(stack_heads(k[pl.ds(k0, KT), cols], masks), qp)
                dp = dot_t(stack_heads(v[pl.ds(k0, KT), cols], masks), gp)
                probs, slopes = [], []
                for side in range(2):
                    h = 2 * hp + side
                    rows = slice(side * KT, (side + 1) * KT)
                    p = jnp.exp(s[rows] + bias - lse[h:h + 1, pl.ds(q0, QT)])
                    slopes.append((p * (dp[rows] - inner[h:h + 1, pl.ds(q0, QT)])).astype(BF))
                    probs.append(p.astype(BF))
                probs, slopes = jnp.concatenate(probs, 0), jnp.concatenate(slopes, 0)
                to_v, to_k = dot(probs, gp), dot(slopes, qp)
                dv_acc[:, cols] += jnp.where(left, to_v[:KT], to_v[KT:])
                dk_acc[:, cols] += jnp.where(left, to_k[:KT], to_k[KT:])
                dqt[cols, pl.ds(q0, QT)] += dot(block_diag(kt[cols, pl.ds(k0, KT)]), slopes)
            return 0

        lax.fori_loop(table[base + 2 * j], table[base + 2 * j + 1], q_tile, 0)
        dk[pl.ds(k0, KT), :] = dk_acc[...].astype(BF)
        dv[pl.ds(k0, KT), :] = dv_acc[...].astype(BF)
        return 0

    lax.fori_loop(0, ROW // KT, k_tile, 0)


def normalize(r, xhat, rstd, at):
    centered = r - jnp.mean(r, -1, keepdims=True)
    spread = jnp.mean(centered * centered, -1, keepdims=True)
    scale = lax.rsqrt(spread + 1e-05)
    out = centered * scale
    xhat[at, :] = out
    rstd[at, :] = jnp.broadcast_to(scale, (out.shape[0], 128))
    return out


def norm_back(dh, xhat, rstd, gain):
    dx = dh * gain
    mean_dx = jnp.mean(dx, -1, keepdims=True)
    mean_xx = jnp.mean(dx * xhat, -1, keepdims=True)
    return rstd[:, 0:1] * (dx - mean_dx - xhat * mean_xx)


def fold(x):
    return jnp.sum(x.reshape(-1, 8, x.shape[-1]), 0)


def forward_kernel(
    tlen, slen, x, mem, win, wout, norms,
    q1, k1, v1, q2, k2, v2, c1, c2, lse1, lse2, xh1, rs1, xh2, rs2,
    trow, tcol, scol, table, vt, acc, peak, tally,
):
    tends, sends = ends_of(tlen), ends_of(slen)
    store_seg(tends, trow, tcol)
    store_seg(sends, trow, scol)
    trow[...] = jnp.broadcast_to(seg_row(tends), (8, ROW))
    store_ranges(table, 0, ranges(tends, tends, True, QT, KT, True))
    store_ranges(table, 8, ranges(tends, sends, False, QT, KT, True))

    def project(at):
        for out, src, w in ((q1, x, 0), (k1, x, 1), (v1, x, 2), (k2, mem, 4), (v2, mem, 5)):
            y = dot(src[at, :], win[w * D:(w + 1) * D, :]).astype(BF)
            out[at, :] = y * BF(0.125) if w == 0 else y

    for_rows(256, project)

    def flip(v):
        for i in range(ROW // 128):
            vt[:, i * 128:(i + 1) * 128] = jnp.transpose(v[i * 128:(i + 1) * 128, :])

    flip(v1)
    attend(q1, k1, vt, tcol, trow, table, 0, True, c1, lse1, acc, peak, tally)

    def middle(at):
        r = x[at, :].astype(F32) + dot(c1[at, :], wout[0:D, :])
        h = normalize(r, xh1, rs1, at) * norms[0:1, :] + norms[3:4, :]
        q2[at, :] = dot(h.astype(BF), win[3 * D:4 * D, :]).astype(BF) * BF(0.125)

    for_rows(256, middle)
    flip(v2)
    attend(q2, k2, vt, scol, trow, table, 8, False, c2, lse2, acc, peak, tally)

    def end(at):
        h = xh1[at, :] * norms[0:1, :] + norms[3:4, :]
        normalize(h + dot(c2[at, :], wout[D:2 * D, :]), xh2, rs2, at)

    for_rows(256, end)


def ffn_kernel(tlen, xh2, cot, up, down, norms, result, dh2, gup, gdown, gnorm, h2b, act, du, dy, pre):
    live_end = ends_of(tlen)[SEGS - 2]
    gnorm[...] = jnp.zeros_like(gnorm)
    block = 256

    def rows(i, _):
        at = pl.ds(pl.multiple_of(i * block, block), block)
        h = xh2[at, :] * norms[1:2, :] + norms[4:5, :]
        hb = h.astype(BF)
        h2b[at, :] = hb
        r3 = h
        for j in range(FF // D):
            cols = slice(j * D, (j + 1) * D)
            u = dot(hb, up[:, cols])
            pre[:, cols] = u
            a = (u / (1.0 + jnp.exp(-u))).astype(BF)
            act[at, cols] = a
            r3 = r3 + dot(a, down[cols, :])
        centered = r3 - jnp.mean(r3, -1, keepdims=True)
        spread = jnp.mean(centered * centered, -1, keepdims=True)
        rstd = lax.rsqrt(spread + 1e-05)
        xhat = centered * rstd
        result[at, :] = (xhat * norms[2:3, :] + norms[5:6, :]).astype(BF)
        place = i * block + lax.broadcasted_iota(jnp.int32, (block, D), 0)
        seed = jnp.where(place < live_end, cot[at, :].astype(F32), 0.0)
        gnorm[0:8, :] += fold(seed * xhat)
        gnorm[8:16, :] += fold(seed)
        dr3 = norm_back(seed, xhat, rstd, norms[2:3, :])
        dyb = dr3.astype(BF)
        dy[at, :] = dyb
        dh = dr3
        for j in range(FF // D):
            cols = slice(j * D, (j + 1) * D)
            da = dot_t(dyb, down[cols, :])
            u = pre[:, cols]
            sig = 1.0 / (1.0 + jnp.exp(-u))
            d = (da * (sig * (1.0 + u * (1.0 - sig)))).astype(BF)
            du[at, cols] = d
            dh = dh + dot_t(d, up[:, cols])
        dh2[at, :] = dh
        return 0

    lax.fori_loop(0, ROW // block, rows, 0)
    for j in range(FF // D):
        cols = slice(j * D, (j + 1) * D)
        gdown[cols, :] = t_dot(act[:, cols], dy[...]).astype(BF)
        gup[:, cols] = t_dot(h2b[...], du[:, cols]).astype(BF)


def backward_kernel(
    tlen, slen, x, mem, win, wout, norms, q1, k1, v1, q2, k2, v2, c1, c2, lse1, lse2, xh1, rs1, xh2, rs2, dh2,
    tgrad, mgrad, gin, gout, gnorm,
    trow, tcol, scol, table, kt, dc, h1b, inner, dqt, dq, dk, dv, dk_acc, dv_acc, dr,
):
    tends, sends = ends_of(tlen), ends_of(slen)
    store_seg(tends, trow, tcol)
    store_seg(sends, trow, scol)
    trow[...] = jnp.broadcast_to(seg_row(tends), (8, ROW))
    store_ranges(table, 0, ranges(tends, tends, True, KT, QT, False))
    store_ranges(table, 16, ranges(tends, sends, False, KT, QT, False))
    gnorm[...] = jnp.zeros_like(gnorm)
    heads = (lax.broadcasted_iota(jnp.int32, (HEADS, D), 1) // HD == lax.broadcasted_iota(jnp.int32, (HEADS, D), 0))
    heads = heads.astype(F32).astype(BF)

    def into_attention(at, r, w, c):
        g = dot_t(r.astype(BF), wout[w * D:(w + 1) * D, :]).astype(BF)
        dc[at, :] = g
        both = g.astype(F32) * c[at, :].astype(F32)
        high = both.astype(BF)
        low = (both - high.astype(F32)).astype(BF)
        inner[:, at] = dot_t(heads, high) + dot_t(heads, low)

    def flip(k):
        for i in range(ROW // 128):
            kt[:, i * 128:(i + 1) * 128] = jnp.transpose(k[i * 128:(i + 1) * 128, :])

    def queries_back(at):
        dq[at, :] = jnp.transpose(dqt[:, at] * 0.125).astype(BF)

    def first(at):
        dh, xhat = dh2[at, :], xh2[at, :]
        gnorm[0:8, :] += fold(dh * xhat)
        gnorm[8:16, :] += fold(dh)
        r = norm_back(dh, xhat, rs2[at, :], norms[1:2, :])
        dr[at, :] = r
        h1b[at, :] = (xh1[at, :] * norms[0:1, :] + norms[3:4, :]).astype(BF)
        into_attention(at, r, 1, c2)

    for_rows(256, first)
    gout[D:2 * D, :] = t_dot(c2[...], dr[...].astype(BF)).astype(BF)
    flip(k2)
    attend_back(q2, k2, v2, kt, dc, lse2, inner, scol, trow, table, 16, False, dqt, dk, dv, dk_acc, dv_acc)
    for_rows(256, queries_back)
    gin[3 * D:4 * D, :] = t_dot(h1b[...], dq[...]).astype(BF)
    gin[4 * D:5 * D, :] = t_dot(mem[...], dk[...]).astype(BF)
    gin[5 * D:6 * D, :] = t_dot(mem[...], dv[...]).astype(BF)

    def second(at):
        mgrad[at, :] = dot_t(dk[at, :], win[4 * D:5 * D, :]) + dot_t(dv[at, :], win[5 * D:6 * D, :])
        dh = dr[at, :] + dot_t(dq[at, :], win[3 * D:4 * D, :])
        xhat = xh1[at, :]
        gnorm[16:24, :] += fold(dh * xhat)
        gnorm[24:32, :] += fold(dh)
        r = norm_back(dh, xhat, rs1[at, :], norms[0:1, :])
        dr[at, :] = r
        into_attention(at, r, 0, c1)

    for_rows(256, second)
    gout[0:D, :] = t_dot(c1[...], dr[...].astype(BF)).astype(BF)
    flip(k1)
    attend_back(q1, k1, v1, kt, dc, lse1, inner, tcol, trow, table, 0, True, dqt, dk, dv, dk_acc, dv_acc)
    for_rows(256, queries_back)
    for i, g in enumerate((dq, dk, dv)):
        gin[i * D:(i + 1) * D, :] = t_dot(x[...], g[...]).astype(BF)

    def third(at):
        t = dr[at, :]
        for i, g in enumerate((dq, dk, dv)):
            t = t + dot_t(g[at, :], win[i * D:(i + 1) * D, :])
        tgrad[at, :] = t

    for_rows(256, third)


VM = pl.BlockSpec(memory_space=pltpu.VMEM)
SM = pl.BlockSpec(memory_space=pltpu.SMEM)


def call(kernel, name, ins, outs, scratch, scalars):
    return pl.pallas_call(
        kernel,
        out_shape=[jax.ShapeDtypeStruct(s, d) for s, d in outs],
        in_specs=[SM] * scalars + [VM] * (len(ins) - scalars),
        out_specs=[VM] * len(outs),
        scratch_shapes=scratch,
        compiler_params=pltpu.CompilerParams(vmem_limit_bytes=62 << 20),
        name=name,
    )(*ins)


def layer(tlen, slen, x, mem, cot, win, wout, up, down, norms):
    tok, tokf, stat, rep = ((ROW, D), BF), ((ROW, D), F32), ((HEADS, ROW), F32), ((ROW, 128), F32)
    segs = [pltpu.VMEM((8, ROW), F32), pltpu.VMEM((ROW, 128), F32), pltpu.VMEM((ROW, 128), F32), pltpu.SMEM((32,), jnp.int32)]
    kept = call(
        forward_kernel, "forward", [tlen, slen, x, mem, win, wout, norms],
        [tok] * 8 + [stat] * 2 + [tokf, rep] * 2,
        segs + [pltpu.VMEM((D, ROW), BF), pltpu.VMEM((D, QT), F32), pltpu.VMEM((HEADS, QT), F32), pltpu.VMEM((HEADS, QT), F32)],
        2,
    )
    xh2 = kept[12]
    result, dh2, gup, gdown, gnorm_three = call(
        ffn_kernel, "feed_forward", [tlen, xh2, cot, up, down, norms],
        [tok, tokf, ((D, FF), BF), ((FF, D), BF), ((16, D), F32)],
        [pltpu.VMEM((ROW, D), BF), pltpu.VMEM((ROW, FF), BF), pltpu.VMEM((ROW, FF), BF), pltpu.VMEM((ROW, D), BF), pltpu.VMEM((256, FF), F32)],
        1,
    )
    tgrad, mgrad, gin, gout, gnorm_rest = call(
        backward_kernel, "backward", [tlen, slen, x, mem, win, wout, norms, *kept, dh2],
        [tokf, tokf, ((6 * D, D), BF), ((2 * D, D), BF), ((32, D), F32)],
        segs + [pltpu.VMEM((D, ROW), BF), pltpu.VMEM((ROW, D), BF), pltpu.VMEM((ROW, D), BF), pltpu.VMEM((HEADS, ROW), F32),
                pltpu.VMEM((D, ROW), F32)] + [pltpu.VMEM((ROW, D), BF)] * 3 + [pltpu.VMEM((KT, D), F32)] * 2 + [pltpu.VMEM((ROW, D), F32)],
        2,
    )
    three = jnp.sum(gnorm_three.reshape(2, 8, D), 1)
    rest = jnp.sum(gnorm_rest.reshape(4, 8, D), 1)
    gnorm = jnp.stack([rest[2], rest[0], three[0], rest[3], rest[1], three[1]])
    return result, tgrad, mgrad, gin, gout, gup, gdown, gnorm


def shard_views(inward, outward, expand, shrink, norms):
    arrays, shapes = [], []
    for x, wide in ((inward, D), (outward, D), (expand, FF), (shrink, D)):
        cols = wide if x.shape[0] >= 16 * wide else D
        arrays.append(x.reshape(-1, 128))
        shapes.append((x.shape[0] // cols, cols))
    width = -(-norms.shape[0] // 128) * 128
    arrays.append(jnp.pad(norms, (0, width - norms.shape[0])).reshape(1, width))
    shapes.append((1, width))
    return arrays, tuple(shapes)


def body(
    sizes, target, memory, cotangent, target_lengths, source_lengths,
    inward_master, inward_mean, inward_square, outward_master, outward_mean, outward_square,
    expand_master, expand_mean, expand_square, shrink_master, shrink_mean, shrink_square,
    norms_master, norms_mean, norms_square,
):
    flat, shapes = shard_views(inward_master, outward_master, expand_master, shrink_master, norms_master)
    win, wout, up, down, norms = gather_all(sizes, flat, shapes, [BF, BF, BF, BF, F32])
    norm_count = norms_master.shape[0]
    norms = norms.reshape(-1, norms.shape[-1])[:, :norm_count].reshape(6, D)
    result, tgrad, mgrad, gin, gout, gup, gdown, gnorm = layer(
        target_lengths, source_lengths, target[0], memory[0], cotangent[0],
        win.reshape(6 * D, D), wout.reshape(2 * D, D), up.reshape(D, FF), down.reshape(FF, D), norms,
    )
    gnorm = jnp.pad(gnorm.reshape(-1, norm_count), ((0, 0), (0, shapes[4][1] - norm_count)))
    grads = [g.reshape(*sizes, *s) for g, s in zip((gin, gout, gup, gdown, gnorm), shapes)]
    means, _ = shard_views(inward_mean, outward_mean, expand_mean, shrink_mean, norms_mean)
    squares, _ = shard_views(inward_square, outward_square, expand_square, shrink_square, norms_square)
    outs = [x.reshape(-1) for x in reduce_all(sizes, grads, means, squares, shapes)]
    return (result[None], tgrad[None], mgrad[None], *outs[:12], *[x[:norm_count] for x in outs[12:]])


def solution(mesh):
    rows, cols = mesh.shape["dp"], mesh.shape["shard"]
    both = ("dp", "shard")
    row, flat = P(both, None, None), P(both)
    return jax.shard_map(
        functools.partial(body, (rows // 2, 2, cols // 2, 2)),
        mesh=mesh,
        in_specs=(row, row, row, P(both, None), P(both, None), *[flat] * 15),
        out_specs=(row, row, row, *[flat] * 15),
        check_vma=False,
    )
```

time: 640 us -> 312 us (0.49); the launches traced: 631 us -> 313 us
  matrix products: 365 us -> 0 us
  Pallas kernels: 136 us -> 283 us
  local copies, waits for them, and re-layouts: 76.6 us -> 28.3 us
  other arithmetic: 36.4 us -> 0.89 us
  loops' own time: 14.8 us -> 0 us
    dot_general x58 -> x0, matrix products: 365 us -> none  [the longest x4 94.5 us: one_block(): jnp.einsum('hqk,qhd->khd', grad_scores, q_block, preferred_element_type=j...]
    pallas_call x0 -> x3, Pallas kernels: none -> 135 us  [call(): pl.pallas_call(kernel, out_shape=[jax.ShapeDtypeStruct(s, d) for s, d in...]
    reduce_sum x13 -> x2, other arithmetic: 24.2 us -> 0.89 us  [the longest x1 0.87 us: layer(): rest = jnp.sum(gnorm_rest.reshape(4, 8, D), 1)]
    another operation x4 -> x0, loops' own time: 14.8 us -> none  [the longest x2 11.2 us: one_row(): lax.scan(one_block, (empty, empty), jnp.arange(block_count, dtype=jnp.int...]
    unnamed x192 -> x40, local copies, waits for them, and re-layouts: 36.3 us -> 22.3 us
    pallas_call x1, Pallas kernels: 84.5 us -> 95.9 us  [reduce_all(): pl.pallas_call(functools.partial(reduce_kernel, mesh_sizes, shapes, [len(...]
    while x24 -> x0, local copies, waits for them, and re-layouts: 10.7 us -> none
    convert_element_type x4 -> x0, local copies, waits for them, and re-layouts: 10.1 us -> none  [the longest x1 2.69 us: body(): ctx_one = ctx_raw.reshape(-1, D).astype(jnp.bfloat16)]
where the time goes in v2:
time: 312 us; the launch traced here: 313 us
  Pallas kernels  283 us (91%)
  local copies, waits for them, and re-layouts  28.3 us (9%)
    pallas_call x3, Pallas kernels, call(): pl.pallas_call(kernel, out_shape=[jax.ShapeDtypeStruct(s, d) for s, d in...  135 us
    pallas_call x1, Pallas kernels, reduce_all(): pl.pallas_call(functools.partial(reduce_kernel, mesh_sizes, shapes, [len(...  95.9 us
    pallas_call x1, Pallas kernels, gather_all(): pl.pallas_call(functools.partial(gather_kernel, mesh_sizes, shapes), out_...  51.9 us
    unnamed x40, local copies, waits for them, and re-layouts  22.3 us

profile of v2, /device:TPU:0, one launch (start us, length us, event | category | flops | bytes accessed | tf_op | source)
XLA Modules:
  0.0 313.2 jit_solution(18185334369552662682)
XLA Ops:
  0.7 0.7 pad_bitcast_fusion.2.refs_4_
  1.3 0.0 copy-start.3
  1.3 0.9 copy-done.3
  2.2 0.0 copy-start.4
  2.2 0.9 copy-done.4
  3.1 0.0 copy-start.5
  3.1 0.9 copy-done.5
  4.1 0.0 copy-start.6
  4.1 0.8 copy-done.6
  4.9 51.9 %gather_weights.1 = (bf16[4,2,2,2,96,512]{5,4,3,2,1,0:T(8,128)(2,1)}, bf16[4,2,2,2,32,512]{5,4,3,2,1,0:T(8,128)(2,1)S(1)}, bf16[4,2,2,2,16,2048]{5,4,3,2,1,0:T(8...) custom-call(f32[384,128]{1,0:T(8,128)S(1)} %bitcast.61, f32[128,128]{1,0:T(8,128)S(1)} %bitcast.64, ...), custom_call_target="tpu_custom_call" | custom-call | tf_op jit(solution)/shard_map/gather_weights/pallas_call | solution.py:193
  56.8 0.0 copy-start
  56.8 1.0 copy-done
  57.8 0.0 copy-start.1
  57.8 1.3 copy-done.1
  59.1 0.0 copy-start.2
  59.1 1.3 copy-done.2
  60.4 0.7 reshape.173.norms
  61.1 51.1 %forward.1 = (bf16[1024,512]{1,0:T(8,128)(2,1)}, bf16[1024,512]{1,0:T(8,128)(2,1)}, bf16[1024,512]{1,0:T(8,128)(2,1)}, bf16[1024,512]{1,0:T(8,128)(2,1)}, bf16[1...) custom-call(s32[1,24]{1,0:T(1,128)} %tlen.5, ...), custom_call_target="tpu_custom_call" | custom-call | tf_op jit(solution)/shard_map/forward/pallas_call | solution.py:780
  112.1 24.3 %feed_forward.1 = (bf16[1024,512]{1,0:T(8,128)(2,1)}, f32[1024,512]{1,0:T(8,128)}, bf16[512,2048]{1,0:T(8,128)(2,1)}, bf16[2048,512]{1,0:T(8,128)(2,1)}, f32[16,512]{1,0:T(8,128)}) custom-call(s32[1,24]{1,0:T(1,128)} %tlen.5, f32[1024,512]{1,0:T(8,128)} %get-tuple-element.65.xh2, bf16[1024,512]{1,0:T(8,128)(2,1)} %bitcast.76, bf16[512,2048]{1,0:T(8,128)(2,1)} %bitcast.59, ...), custom_call_target="tpu_custom_call" | custom-call | tf_op jit(solution)/shard_map/feed_forward/pallas_call | solution.py:780
  136.4 0.0 copy-start.11
  136.4 0.0 copy-start.12
  136.4 0.0 copy-start.13
  136.4 60.1 %backward.1 = (f32[1024,512]{1,0:T(8,128)}, f32[1024,512]{1,0:T(8,128)}, bf16[3072,512]{1,0:T(8,128)(2,1)}, bf16[1024,512]{1,0:T(8,128)(2,1)}, f32[32,512]{1,0:T(8,128)}) custom-call(s32[1,24]{1,0:T(1,128)} %tlen.5, s32[1,24]{1,0:T(1,128)} %slen.3, bf16[1024,512]{1,0:T(8,128)(2,1)} %bitcast.69, bf16[1024,512]{1,0:T(8,128)(2,1)} %bitcast.71, ...), custom_call_target="tpu_custom_call" | custom-call | tf_op jit(solution)/shard_map/backward/pallas_call | solution.py:780
  196.5 0.9 bitcast_reduce_fusion
  197.4 0.0 copy-done.11
  197.5 0.1 reshape.182
  197.6 0.6 pad.15
  198.2 0.0 copy-done.12
  198.2 0.0 copy-done.13
  198.2 0.5 pad_bitcast_fusion
  198.7 95.9 %reduce_gradients.1 = (f32[384,128]{1,0:T(8,128)}, f32[384,128]{1,0:T(8,128)}, f32[384,128]{1,0:T(8,128)}, f32[128,128]{1,0:T(8,128)}, f32[128,128]{1,0:T(8,128)...) custom-call(bf16[4,2,2,2,96,512]{5,4,3,2,1,0:T(8,128)(2,1)} %bitcast, ...), custom_call_target="tpu_custom_call" | custom-call | tf_op jit(solution)/shard_map/reduce_gradients/pallas_call | solution.py:370
  294.6 0.0 copy-start.10
  294.6 0.0 copy-start.9
  294.6 0.0 copy-start.8
  294.6 0.0 copy-start.7
  294.6 1.2 slice_bitcast_fusion
  295.8 1.2 slice_bitcast_fusion.1
  297.0 1.1 slice_bitcast_fusion.2
  298.1 1.6 copy.50
  299.7 1.6 copy.51
  301.3 1.6 copy.52
  302.9 1.5 copy.53
  304.4 1.5 copy.54
  305.9 1.5 copy.55
  307.4 1.6 copy.56
  308.9 1.6 copy.57
  310.5 0.0 copy-done.10
  310.5 0.7 copy.58
  311.2 0.0 copy-done.9
  311.2 0.7 copy.59
  311.8 0.0 copy-done.8
  311.8 0.7 copy.60
  312.5 0.0 copy-done.7
  312.5 0.7 copy.61
  (3 shorter events, 0.1 us)
Async XLA Ops:
  1.3 0.9 copy-start.3
  2.2 0.9 copy-start.4
  3.1 0.9 copy-start.5
  4.1 0.8 copy-start.6
  56.8 1.0 copy-start
  57.8 1.3 copy-start.1
  59.1 1.3 copy-start.2
  136.4 61.0 %copy-start.11 = (f32[16,512]{1,0:T(8,128)S(1)}, f32[16,512]{1,0:T(8,128)}, u32[]{:S(2)}) copy-start(f32[16,512]{1,0:T(8,128)} %get-tuple-element.90) | copy-start | bytes 98308
  136.4 61.8 %copy-start.12 = (f32[96]{0:T(128)S(1)}, f32[96]{0:T(128)}, u32[]{:S(2)}) copy-start(f32[96]{0:T(128)} %param.39) | copy-start | bytes 1156
  136.4 61.8 %copy-start.13 = (f32[96]{0:T(128)S(1)}, f32[96]{0:T(128)}, u32[]{:S(2)}) copy-start(f32[96]{0:T(128)} %param.38) | copy-start | bytes 1156
  294.6 15.9 %copy-start.10 = (f32[256,128]{1,0:T(8,128)S(1)}, f32[256,128]{1,0:T(8,128)}, u32[]{:S(2)}) copy-start(f32[256,128]{1,0:T(8,128)} %get-tuple-element.99) | copy-start | bytes 393220
  294.6 16.6 %copy-start.9 = (f32[256,128]{1,0:T(8,128)S(1)}, f32[256,128]{1,0:T(8,128)}, u32[]{:S(2)}) copy-start(f32[256,128]{1,0:T(8,128)} %get-tuple-element.100) | copy-start | bytes 393220
  294.6 17.2 %copy-start.8 = (f32[256,128]{1,0:T(8,128)S(1)}, f32[256,128]{1,0:T(8,128)}, u32[]{:S(2)}) copy-start(f32[256,128]{1,0:T(8,128)} %get-tuple-element.101) | copy-start | bytes 393220
  294.6 17.9 %copy-start.7 = (f32[256,128]{1,0:T(8,128)S(1)}, f32[256,128]{1,0:T(8,128)}, u32[]{:S(2)}) copy-start(f32[256,128]{1,0:T(8,128)} %get-tuple-element.102) | copy-start | bytes 393220

commit v3 on v2

--- a/solution.py
+++ b/solution.py
@@ -162,7 +162,157 @@
         dst[pl.ds(j, rows, stride=w), :] = value[:, j * 128:(j + 1) * 128]
 
 
+MOST_PATHS = 40
+
+
+def both(a, b):
+    return b if a is None else a if b is None else a & b
+
+
+def when(cond, f):
+    if cond is None:
+        f()
+    else:
+        pl.when(cond)(f)
+
+
+def paths(order, sizes):
+    found = [()]
+    for axis in order:
+        n = sizes[axis]
+        moves = [(axis, 0, 1)] if n == 2 else [(axis, way, d) for d in range(1, n) for way in (1, -1)]
+        found = found + [p + (m,) for p in found for m in moves]
+    return sorted(found, key=lambda p: sum(m[2] for m in p))
+
+
+def parent(path):
+    axis, way, dist = path[-1]
+    return path[:-1] + (((axis, way, dist - 1),) if dist > 1 else ())
+
+
+class Block:
+    def __init__(self, place, path):
+        self.coords, self.exists = list(place.at), None
+        for axis, way, dist in path:
+            me, n = place.at[axis], place.sizes[axis]
+            self.coords[axis] = 1 - me if way == 0 else me - way * dist
+            if way:
+                self.exists = both(self.exists, (self.coords[axis] >= 0) & (self.coords[axis] < n))
+
+    def next_hop(self, place, child):
+        axis, way, _ = child[-1]
+        me, n = place.at[axis], place.sizes[axis]
+        to = 1 - me if way == 0 else me + way
+        ok = None if way == 0 else (to >= 0) & (to < n)
+        return place.device(axis, to), both(self.exists, ok)
+
+
+def remote(src, dst, pair, device):
+    return pltpu.make_async_remote_copy(
+        src_ref=src, dst_ref=dst, send_sem=pair[0], recv_sem=pair[1], device_id=device, device_id_type=MESH)
+
+
+def gather_flow(place, ref, order, sems):
+    e, sibling = place.at[3], place.device(3, 1 - place.at[3])
+    ways = paths(order, place.sizes)
+    blocks = {p: Block(place, p) for p in ways}
+    pairs = {p: sems.take() for p in ways if p}
+    after = []
+    for p in ways:
+        b = blocks[p]
+        mine = ref.at[tuple(b.coords)]
+        if p:
+            yield
+            when(b.exists, remote(mine, mine, pairs[p], sibling).wait_recv)
+        for child in ways:
+            if child and parent(child) == p:
+                device, ok = b.next_hop(place, child)
+                go = remote(mine, mine, pairs[child], device)
+                when(ok, go.start)
+                after.append((ok, go.wait_send))
+        pair = sems.take()
+        go = remote(mine, mine, pair, sibling)
+        theirs = ref.at[(*b.coords[:3], 1 - e)]
+        come = remote(theirs, theirs, pair, sibling)
+        when(b.exists, go.start)
+        after.append((b.exists, go.wait_send))
+        after.append((b.exists, come.wait_recv))
+    yield
+    for ok, f in after:
+        when(ok, f)
+
+
+def reduce_flow(place, grad, order, half, arrived, total, sems):
+    e, sibling = place.at[3], place.device(3, 1 - place.at[3])
+    ways = paths(order, place.sizes)[::-1]
+    blocks = {p: Block(place, p) for p in ways}
+    slot = {p: i for i, p in enumerate(p for p in ways if p)}
+    pairs = {p: sems.take() for p in ways if p}
+    cores = {p: sems.take() for p in ways}
+    rows = total.shape[0]
+    chunk = 32 if rows % 32 == 0 else 16 if rows % 16 == 0 else rows
+    after = []
+    for p in ways:
+        b = blocks[p]
+        go = remote(grad.at[(*b.coords[:3], 1 - e)], half.at[tuple(b.coords[:3])], cores[p], sibling)
+        when(b.exists, go.start)
+        after.append((b.exists, go.wait_send))
+    for p in ways:
+        yield
+        b = blocks[p]
+        own, sums = grad.at[tuple(b.coords)], half.at[tuple(b.coords[:3])]
+        kids = []
+        for child in ways:
+            if child and parent(child) == p:
+                device, ok = b.next_hop(place, child)
+                here = arrived.at[slot[child]]
+                when(ok, remote(here, here, pairs[child], device).wait_recv)
+                kids.append((here, ok))
+        when(b.exists, remote(own, sums, cores[p], sibling).wait_recv)
+
+        def add():
+            def step(i, _):
+                at = pl.ds(pl.multiple_of(i * chunk, chunk), chunk)
+                v = own[at, :].astype(F32) + sums[at, :].astype(F32)
+                for here, ok in kids:
+                    term = here[at, :].astype(F32)
+                    v = v + (term if ok is None else jnp.where(ok, term, 0.0))
+                if p:
+                    sums[at, :] = v.astype(sums.dtype)
+                else:
+                    total[at, :] = v
+                return 0
+
+            if rows == chunk:
+                v = own[...].astype(F32) + sums[...].astype(F32)
+                for here, ok in kids:
+                    term = here[...].astype(F32)
+                    v = v + (term if ok is None else jnp.where(ok, term, 0.0))
+                if p:
+                    sums[...] = v.astype(sums.dtype)
+                else:
+                    total[...] = v
+            else:
+                lax.fori_loop(0, rows // chunk, step, 0)
+
+        when(b.exists, add)
+        if p:
+            axis, way, _ = p[-1]
+            me = place.at[axis]
+            device = place.device(axis, 1 - me if way == 0 else me - way)
+            go = remote(sums, arrived.at[slot[p]], pairs[p], device)
+            when(b.exists, go.start)
+            after.append((b.exists, go.wait_send))
+    yield
+    for ok, f in after:
+        when(ok, f)
+
+
 ORDERS = ((0, 2, 1), (0, 1, 2), (1, 2, 0), (0, 1, 2), (0, 1, 2))
+
+
+def flows(sizes):
+    return len(paths((0, 1, 2), sizes)) <= MOST_PATHS
 
 
 def gather_kernel(sizes, shapes, *refs):
@@ -183,12 +333,16 @@
     for cp in copies:
         cp.wait()
     sems = Sems(send, recv)
-    interleave([gather_rounds(place, outs[k], ORDERS[k], sems) for k in range(n)])
+    rounds = gather_flow if flows(sizes) else gather_rounds
+    interleave([rounds(place, outs[k], ORDERS[k], sems) for k in range(n)])
 
 
 def gather_all(mesh_sizes, masters, shapes, dtypes):
     n = len(shapes)
-    total = sum(gather_sems(ORDERS[k], mesh_sizes) for k in range(n))
+    if flows(mesh_sizes):
+        total = n * 2 * len(paths((0, 1, 2), mesh_sizes))
+    else:
+        total = sum(gather_sems(ORDERS[k], mesh_sizes) for k in range(n))
     vm = pl.BlockSpec(memory_space=pltpu.VMEM)
     return pl.pallas_call(
         functools.partial(gather_kernel, mesh_sizes, shapes),
@@ -339,42 +493,63 @@
         del refs[:k]
         return out
 
-    grads, means, squares = take(n), take(n), take(n)
-    outs = take(3 * n)
-    totals = take(n)
+    grads, totals = take(n), take(n)
     bufs = [take(c) for c in counts]
     send, recv = take(2)
     place = Place(sizes)
     place.greet()
     sems = Sems(send, recv)
-    interleave([reduce_rounds(place, grads[k], BACK[k], bufs[k][0], bufs[k][1:], totals[k], sems) for k in range(n)])
-    for k, (rows, cols) in enumerate(shapes):
-        change, mean, summed = outs[3 * k:3 * k + 3]
-        if rows == 1:
-            summed[...] = totals[k][...]
-        else:
-            rows_to_flat(totals[k], summed, rows, cols)
-        change[...], mean[...] = adam(means[k][...], squares[k][...], summed[...])
-
-
-def reduce_all(mesh_sizes, grads, means, squares, shapes):
+    if flows(sizes):
+        interleave([reduce_flow(place, grads[k], ORDERS[k], *bufs[k], totals[k], sems) for k in range(n)])
+    else:
+        interleave([reduce_rounds(place, grads[k], BACK[k], bufs[k][0], bufs[k][1:], totals[k], sems) for k in range(n)])
+
+
+def reduce_all(mesh_sizes, grads, shapes):
     n = len(shapes)
-    flat = [((s[0] * s[1]) // 128, 128) for s in shapes]
-    lists = [reduce_bufs(BACK[k], mesh_sizes, shapes[k]) for k in range(n)]
-    total = sum(reduce_sems(BACK[k], mesh_sizes) for k in range(n))
+    ways = len(paths((0, 1, 2), mesh_sizes))
+    if flows(mesh_sizes):
+        lists = [[(*mesh_sizes[:3], *s), (ways - 1, *s)] for s in shapes]
+        total = n * 2 * ways
+    else:
+        lists = [reduce_bufs(BACK[k], mesh_sizes, shapes[k]) for k in range(n)]
+        total = sum(reduce_sems(BACK[k], mesh_sizes) for k in range(n))
     vm = pl.BlockSpec(memory_space=pltpu.VMEM)
-    scratch = [pltpu.VMEM(s, F32) for s in shapes]
+    scratch = []
     for k in range(n):
         scratch += [pltpu.VMEM(s, grads[k].dtype) for s in lists[k]]
     scratch += [pltpu.SemaphoreType.DMA((total,)), pltpu.SemaphoreType.DMA((total,))]
     return pl.pallas_call(
         functools.partial(reduce_kernel, mesh_sizes, shapes, [len(x) for x in lists]),
-        out_shape=[jax.ShapeDtypeStruct(f, F32) for f in flat for _ in range(3)],
-        in_specs=[vm] * (3 * n),
-        out_specs=[vm] * (3 * n),
+        out_shape=[jax.ShapeDtypeStruct(s, F32) for s in shapes],
+        in_specs=[vm] * n,
+        out_specs=[vm] * n,
         scratch_shapes=scratch,
         compiler_params=pltpu.CompilerParams(collective_id=1, has_side_effects=True, vmem_limit_bytes=60 << 20),
         name="reduce_gradients",
+    )(*grads)
+
+
+def adam_kernel(shapes, *refs):
+    n = len(shapes)
+    grads, means, squares, outs = refs[:n], refs[n:2 * n], refs[2 * n:3 * n], refs[3 * n:]
+    for k, (rows, cols) in enumerate(shapes):
+        change, mean, summed = outs[3 * k:3 * k + 3]
+        if rows == 1:
+            summed[...] = grads[k][...]
+        else:
+            rows_to_flat(grads[k], summed, rows, cols)
+        change[...], mean[...] = adam(means[k][...], squares[k][...], summed[...])
+
+
+def adam_all(grads, means, squares, shapes):
+    vm = pl.BlockSpec(memory_space=pltpu.VMEM)
+    return pl.pallas_call(
+        functools.partial(adam_kernel, shapes),
+        out_shape=[jax.ShapeDtypeStruct(((r * c) // 128, 128), F32) for r, c in shapes for _ in range(3)],
+        in_specs=[vm] * (3 * len(shapes)),
+        out_specs=[vm] * (3 * len(shapes)),
+        name="adam",
     )(*grads, *means, *squares)
 
 
@@ -847,7 +1022,8 @@
     grads = [g.reshape(*sizes, *s) for g, s in zip((gin, gout, gup, gdown, gnorm), shapes)]
     means, _ = shard_views(inward_mean, outward_mean, expand_mean, shrink_mean, norms_mean)
     squares, _ = shard_views(inward_square, outward_square, expand_square, shrink_square, norms_square)
-    outs = [x.reshape(-1) for x in reduce_all(sizes, grads, means, squares, shapes)]
+    sums = reduce_all(sizes, grads, shapes)
+    outs = [x.reshape(-1) for x in adam_all(sums, means, squares, shapes)]
     return (result[None], tgrad[None], mgrad[None], *outs[:12], *[x[:norm_count] for x in outs[12:]])
 
 

time: 312 us -> 253 us (0.81)
  Pallas kernels: 283 us -> 239 us
  local copies, waits for them, and re-layouts: 28.3 us -> 13.2 us
    pallas_call x1, Pallas kernels: 95.9 us -> 62 us  [reduce_all(): pl.pallas_call(functools.partial(reduce_kernel, mesh_sizes, shapes, [len(...]
    unnamed x40 -> x20, local copies, waits for them, and re-layouts: 22.3 us -> 7.21 us
    pallas_call x3, Pallas kernels: 135 us -> 129 us  [call(): pl.pallas_call(kernel, out_shape=[jax.ShapeDtypeStruct(s, d) for s, d in...]
    pallas_call x1, Pallas kernels: 51.9 us -> 45.1 us  [gather_all(): pl.pallas_call(functools.partial(gather_kernel, mesh_sizes, shapes), out_...]
where the time goes in v3:
time: 253 us
  Pallas kernels  239 us (94%)
  local copies, waits for them, and re-layouts  13.2 us (5%)
    pallas_call x3, Pallas kernels, call(): pl.pallas_call(kernel, out_shape=[jax.ShapeDtypeStruct(s, d) for s, d in...  129 us
    pallas_call x1, Pallas kernels, reduce_all(): pl.pallas_call(functools.partial(reduce_kernel, mesh_sizes, shapes, [len(...  62 us
    pallas_call x1, Pallas kernels, gather_all(): pl.pallas_call(functools.partial(gather_kernel, mesh_sizes, shapes), out_...  45.1 us
    unnamed x20, local copies, waits for them, and re-layouts  7.21 us

profile of v3, /device:TPU:0, one launch (start us, length us, event | category | flops | bytes accessed | tf_op | source)
XLA Modules:
  0.0 253.4 jit_solution(13789672676916352471)
XLA Ops:
  0.7 0.7 pad_bitcast_fusion.2.refs_4_
  1.3 0.0 copy-start.3
  1.3 0.9 copy-done.3
  2.2 0.0 copy-start.4
  2.2 0.9 copy-done.4
  3.1 0.0 copy-start.5
  3.1 0.9 copy-done.5
  4.1 0.0 copy-start.6
  4.1 0.8 copy-done.6
  4.9 45.1 %gather_weights.1 = (bf16[4,2,2,2,96,512]{5,4,3,2,1,0:T(8,128)(2,1)}, bf16[4,2,2,2,32,512]{5,4,3,2,1,0:T(8,128)(2,1)S(1)}, bf16[4,2,2,2,16,2048]{5,4,3,2,1,0:T(8...) custom-call(f32[384,128]{1,0:T(8,128)S(1)} %bitcast.61, f32[128,128]{1,0:T(8,128)S(1)} %bitcast.64, ...), custom_call_target="tpu_custom_call" | custom-call | tf_op jit(solution)/shard_map/gather_weights/pallas_call | solution.py:347
  50.0 0.0 copy-start
  50.0 1.0 copy-done
  51.0 0.0 copy-start.1
  51.0 1.3 copy-done.1
  52.3 0.0 copy-start.2
  52.3 1.3 copy-done.2
  53.6 0.7 reshape.173.norms
  54.3 47.6 %forward.1 = (bf16[1024,512]{1,0:T(8,128)(2,1)}, bf16[1024,512]{1,0:T(8,128)(2,1)}, bf16[1024,512]{1,0:T(8,128)(2,1)}, bf16[1024,512]{1,0:T(8,128)(2,1)}, bf16[1...) custom-call(s32[1,24]{1,0:T(1,128)} %tlen.5, ...), custom_call_target="tpu_custom_call" | custom-call | tf_op jit(solution)/shard_map/forward/pallas_call | solution.py:955
  101.9 24.2 %feed_forward.1 = (bf16[1024,512]{1,0:T(8,128)(2,1)}, f32[1024,512]{1,0:T(8,128)}, bf16[512,2048]{1,0:T(8,128)(2,1)}, bf16[2048,512]{1,0:T(8,128)(2,1)}, f32[16,512]{1,0:T(8,128)}) custom-call(s32[1,24]{1,0:T(1,128)} %tlen.5, f32[1024,512]{1,0:T(8,128)} %get-tuple-element.70.xh2, bf16[1024,512]{1,0:T(8,128)(2,1)} %bitcast.75, bf16[512,2048]{1,0:T(8,128)(2,1)} %bitcast.59, ...), custom_call_target="tpu_custom_call" | custom-call | tf_op jit(solution)/shard_map/feed_forward/pallas_call | solution.py:955
  126.2 0.0 copy-start.7
  126.2 56.9 %backward.1 = (f32[1024,512]{1,0:T(8,128)}, f32[1024,512]{1,0:T(8,128)}, bf16[3072,512]{1,0:T(8,128)(2,1)}, bf16[1024,512]{1,0:T(8,128)(2,1)}, f32[32,512]{1,0:T(8,128)}) custom-call(s32[1,24]{1,0:T(1,128)} %tlen.5, s32[1,24]{1,0:T(1,128)} %slen.3, bf16[1024,512]{1,0:T(8,128)(2,1)} %bitcast.69, bf16[1024,512]{1,0:T(8,128)(2,1)} %bitcast.71, ...), custom_call_target="tpu_custom_call" | custom-call | tf_op jit(solution)/shard_map/backward/pallas_call | solution.py:955
  183.0 0.9 bitcast_reduce_fusion
  183.9 0.0 copy-done.7
  184.0 0.1 reshape.182
  184.1 0.6 pad.15
  184.7 0.0 copy-start.8
  184.7 0.0 copy-start.9
  184.7 62.0 %reduce_gradients.1 = (f32[96,512]{1,0:T(8,128)}, f32[32,512]{1,0:T(8,128)}, f32[16,2048]{1,0:T(8,128)}, f32[64,512]{1,0:T(8,128)}, f32[1,128]{1,0:T(1,128)}) custom-call(bf16[4,2,2,2,96,512]{5,4,3,2,1,0:T(8,128)(2,1)} %bitcast.72, bf16[4,2,2,2,32,512]{5,4,3,2,1,0:T(8,128)(2,1)} %bitcast.76, bf16[4,2,2,2,16,2048]{5,4,3,2,1,0:T(8,128)(2,1)} %bitcast.73, ...), custom_call_target="tpu_custom_call" | custom-call | tf_op jit(solution)/shard_map/reduce_gradients/pallas_call | solution.py:522
  246.7 0.0 copy-done.8
  246.7 0.0 copy-done.9
  246.7 0.5 pad_bitcast_fusion
  247.2 2.8 %adam.1 = (f32[384,128]{1,0:T(8,128)}, f32[384,128]{1,0:T(8,128)}, f32[384,128]{1,0:T(8,128)}, f32[128,128]{1,0:T(8,128)}, f32[128,128]{1,0:T(8,128)}, /*index=5...) custom-call(f32[96,512]{1,0:T(8,128)} %get-tuple-element.96.refs_0_,, ...), custom_call_target="tpu_custom_call" | custom-call | tf_op jit(solution)/shard_map/adam/pallas_call | solution.py:547
  250.0 1.1 slice_bitcast_fusion
  251.1 1.2 slice_bitcast_fusion.1
  252.3 1.1 slice_bitcast_fusion.2
  (3 shorter events, 0.1 us)
Async XLA Ops:
  1.3 0.9 copy-start.3
  2.2 0.9 copy-start.4
  3.1 0.9 copy-start.5
  4.1 0.8 copy-start.6
  50.0 1.0 copy-start
  51.0 1.3 copy-start.1
  52.3 1.3 copy-start.2
  126.2 57.7 %copy-start.7 = (f32[16,512]{1,0:T(8,128)S(1)}, f32[16,512]{1,0:T(8,128)}, u32[]{:S(2)}) copy-start(f32[16,512]{1,0:T(8,128)} %get-tuple-element.95) | copy-start | bytes 98308
  184.7 62.0 %copy-start.8 = (f32[96]{0:T(128)S(1)}, f32[96]{0:T(128)}, u32[]{:S(2)}) copy-start(f32[96]{0:T(128)} %param.39) | copy-start | bytes 1156
  184.7 62.0 %copy-start.9 = (f32[96]{0:T(128)S(1)}, f32[96]{0:T(128)}, u32[]{:S(2)}) copy-start(f32[96]{0:T(128)} %param.38) | copy-start | bytes 1156
